TPU v7x, 256 devices: a whole 4x4x8 slice. The times are simulated.
256 devices in a mesh: grp: 8 (over y, core), rows: 32 (over z, x).
Axes of the slice: x: 4, y: 4, z: 8, core: 2. Of those that a mesh axis runs over, the one named last changes fastest.
Arguments:
- rhs: float32 [16384, 64, 128], P(('grp', 'rows')), may hold values from -6 to 6
- fine_diag: bfloat16 [16384, 64, 64], P(('grp', 'rows')), may hold values from -0.2 to 1.2
- fine_smoother: bfloat16 [16384, 64, 64], P(('grp', 'rows')), may hold values from -4 to 4
- fine_blocks: bfloat16 [16384, 7, 64, 64], P(('grp', 'rows')), may hold values from -0.1796875 to 0.1796875
- fine_cols: int32 [16384, 7], P(('grp', 'rows')), may hold values from 0 to 16383, as said below
- aggregate: int32 [16384], P(('grp', 'rows')), may hold values from 0 to 2047, as said below
- coarse_diag: bfloat16 [2048, 64, 64], P('rows'), may hold values from -0.8 to 4.8
- coarse_smoother: bfloat16 [2048, 64, 64], P('rows'), may hold values from -1 to 1
- coarse_blocks: bfloat16 [2048, 7, 64, 64], P('rows'), may hold values from -0.71875 to 0.71875
- coarse_cols: int32 [2048, 7], P('rows'), may hold values from 0 to 2047, as said below
Outputs:
- solution: float32 [16384, 64, 128], P(('grp', 'rows'))
Inputs may be any that keep to these rules, and one draw needn't show every extreme that they name: fine_cols row i names rows within 32 of i; the distance 32 is reached. coarse_cols row c names rows within 32 of c; the distance 32 is reached. `aggregate`: aggregate_i lies in [r * 64, (r + 1) * 64) with r = (i // 64) mod 32.
All inputs are finite; a program needn't handle non-finite values.
Results may differ from a plain program's by a relative error of at most 0.001.
The roundings to bfloat16 on the way count: a program that leaves them out, or rounds other values in their place, can miss the bound.
Values may be sent and summed in bfloat16 or wider, within the bound.
No kernel may reach another device: no remote copies, remote signals or barrier semaphores. Data moves between devices by JAX's collectives and lax.ppermute only.
A program may use at most 128 MiB of HBM per device.

v0:
```python
import jax
import jax.numpy as jnp
from jax import lax
from jax.sharding import PartitionSpec as P

damping = 0.8


def extended_2(cells, sides, width):
    for axis, dim in sides:
        count = lax.axis_size(axis)
        ends = count - 1
        head = lax.slice_in_dim(cells, 0, width, axis=dim)
        tail = lax.slice_in_dim(cells, cells.shape[dim] - width, cells.shape[dim], axis=dim)
        cells = jnp.concatenate(
            [
                lax.ppermute(tail, axis, [(i, (i + 1) % count) for i in range(ends)]),
                cells,
                lax.ppermute(head, axis, [((i + 1) % count, i) for i in range(ends)]),
            ],
            axis=dim,
        )
    return cells


def block_product(blocks, vector):
    return jnp.einsum(
        "nab,nbk->nak", blocks, vector.astype(jnp.bfloat16), preferred_element_type=jnp.float32
    )


def nearby_product(off_blocks, columns, extended, first_row):
    nearby = jnp.take(extended, columns - first_row, axis=0)
    return jnp.einsum("njab,njbk->nak", off_blocks, nearby, preferred_element_type=jnp.float32)


def fine_operator(fine_diag, fine_blocks, fine_cols, vector):
    rounded_rows = vector.astype(jnp.bfloat16)
    height = vector.shape[0]
    margin = height // 2
    extended = extended_2(rounded_rows, ((("grp", "rows"), 0),), margin)
    first_row = lax.axis_index(("grp", "rows")) * height - margin
    return block_product(fine_diag, rounded_rows) + nearby_product(
        fine_blocks, fine_cols, extended, first_row
    )


def coarse_nearby(off_blocks, columns, rounded_full):
    height = rounded_full.shape[0]
    margin = height // 2
    extended = extended_2(rounded_full, (("rows", 0),), margin)
    first_row = lax.axis_index("rows") * height - margin
    return nearby_product(off_blocks, columns, extended, first_row)


def on_device(
    rhs,
    fine_diag,
    fine_smoother,
    fine_blocks,
    fine_cols,
    aggregate,
    coarse_diag,
    coarse_smoother,
    coarse_blocks,
    coarse_cols,
):
    first_iterate = damping * block_product(fine_smoother, rhs)
    first_residual = rhs - fine_operator(fine_diag, fine_blocks, fine_cols, first_iterate)
    second_iterate = first_iterate + damping * block_product(fine_smoother, first_residual)
    second_residual = rhs - fine_operator(fine_diag, fine_blocks, fine_cols, second_iterate)
    coarse_height = coarse_diag.shape[0]
    local_index = aggregate - lax.axis_index("rows") * coarse_height
    selector = (local_index[:, None] == jnp.arange(coarse_height, dtype=jnp.int32)[None, :]).astype(
        jnp.float32
    )
    partial_sum = jnp.einsum(
        "fc,fak->cak", selector, second_residual, precision=lax.Precision.HIGHEST
    )
    coarse_rhs = lax.psum(partial_sum, "grp")
    coarse_first = damping * block_product(coarse_smoother, coarse_rhs)
    rounded_first = coarse_first.astype(jnp.bfloat16)
    coarse_image = block_product(coarse_diag, rounded_first) + coarse_nearby(
        coarse_blocks, coarse_cols, rounded_first
    )
    coarse_second = coarse_first + damping * block_product(
        coarse_smoother, coarse_rhs - coarse_image
    )
    return second_iterate + jnp.take(coarse_second, local_index, axis=0)


def solution(mesh):
    in_specs = (
        P(("grp", "rows"), None, None),
        P(("grp", "rows"), None, None),
        P(("grp", "rows"), None, None),
        P(("grp", "rows"), None, None, None),
        P(("grp", "rows"), None),
        P(("grp", "rows")),
        P("rows", None, None),
        P("rows", None, None),
        P("rows", None, None, None),
        P("rows", None),
    )
    out_specs = P(("grp", "rows"), None, None)
    return jax.shard_map(
        on_device, mesh=mesh, in_specs=in_specs, out_specs=out_specs, check_vma=False
    )
```

profile of v0, /device:TPU:129, one launch (start us, length us, event | category | flops | bytes accessed | tf_op | source)
XLA Modules:
  0.0 243.9 jit_solution(1312586477783933816)
XLA Ops:
  7.8 3.4 %multiply_convert_fusion.1 = (bf16[64,64,128]{2,1,0:T(8,128)(2,1)S(1)}, f32[64,64,128]{2,1,0:T(8,128)}) fusion(bf16[64,64,64]{2,1,0:T(8,128)(2,1)S(1)} %copy-done, f32[64,64,128]{2,1,0:T(8,128)} %param.12), kind=kOutput, calls=%fused_computation.33 | convolution fusion | flops 68681728 | bytes 5767168 | tf_op jit(solution)/shard_map/nab,nbk->nak/dot_general | solution.py:27
  12.2 4.0 %collective-permute-start.1 = (bf16[32,64,128]{2,1,0:T(8,128)(2,1)}, bf16[32,64,128]{2,1,0:T(8,128)(2,1)}, u32[]{:S(2)}, u32[]{:S(2)}) collective-permute-start(bf16[32,64,128]{2,1,0:T(8,128)(2,1)} %get-tuple-element.17), channel_id=1, source_target_pairs={{1,0},{2,1},{3,2},{4,3},{5,4},{6,5},{7,6},{8,7},{9,8},{10,9},{11,1... | collective-permute-start | bytes 1572872 | tf_op jit(solution)/shard_map/ppermute | solution.py:19
  16.2 1.9 collective-permute-start
  18.6 1.8 fusion.43
  20.4 6.9 %collective-permute-done.1 = bf16[32,64,128]{2,1,0:T(8,128)(2,1)} collective-permute-done((bf16[32,64,128]{2,1,0:T(8,128)(2,1)}, bf16[32,64,128]{2,1,0:T(8,128)(2,1)}, u32[]{:S(2)}, u32[]{:S(2)}) %collective-permute-start.1) | collective-permute-done | bytes 524320 | tf_op jit(solution)/shard_map/ppermute | solution.py:19
  27.3 6.9 %collective-permute-done = bf16[32,64,128]{2,1,0:T(8,128)(2,1)} collective-permute-done((bf16[32,64,128]{2,1,0:T(8,128)(2,1)}, bf16[32,64,128]{2,1,0:T(8,128)(2,1)}, u32[]{:S(2)}, u32[]{:S(2)}) %collective-permute-start) | collective-permute-done | bytes 524320 | tf_op jit(solution)/shard_map/ppermute | solution.py:17
  34.2 1.8 pad_maximum_fusion
  36.0 13.3 %gather_fusion.1 = bf16[448,64,128]{2,1,0:T(8,128)(2,1)} fusion(bf16[128,64,128]{2,1,0:T(8,128)(2,1)S(1)} %pad_maximum_fusion, s32[1024]{0:T(1024)S(1)} %pad_clamp_fusion.2), kind=kCustom, calls=%fused_computation.clone | custom fusion | bytes 14681856 | tf_op jit(solution)/shard_map/jit(_take)/gather | solution.py:33
  49.3 10.1 %fusion.40 = (bf16[64,64,128]{2,1,0:T(8,128)(2,1)S(1)}, f32[64,64,128]{2,1,0:T(8,128)}) fusion(bf16[64,64,64]{2,1,0:T(8,128)(2,1)S(1)} %copy-done, f32[64,64,128]{2,1,0:T(8,128)} %param.12, f32[64,128,64]{1,2,0:T(8,128)} %fusion.43, bf16[64,7,64,64]{3,2,1,0:T(8,128)(2,1)} %param.15, bf16[64,7,64,128]{3,2,1,0:T(8,128)(2,1)} %bitcast.56, ...), kind=kOutput, calls=%fused_computation.61 | convolution fusion | flops 544210944 | bytes 20971968 | tf_op jit(solution)/shard_map/nab,nbk->nak/dot_general | solution.py:27
  59.5 2.1 collective-permute-start.3
  61.6 3.5 %collective-permute-start.2 = (bf16[32,64,128]{2,1,0:T(8,128)(2,1)S(1)}, bf16[32,64,128]{2,1,0:T(8,128)(2,1)S(1)}, u32[]{:S(2)}, u32[]{:S(2)}) collective-permute-start(bf16[32,64,128]{2,1,0:T(8,128)(2,1)S(1)} %get-tuple-element.14), channel_id=1, source_target_pairs={{0,1},{1,2},{2,3},{3,4},{4,5},{5,6},{6,7},{7,8},{8,9},{9,10},{10,1... | collective-permute-start | bytes 1572872 | tf_op jit(solution)/shard_map/ppermute | solution.py:17
  65.1 1.8 fusion.44
  67.0 6.1 %collective-permute-done.3 = bf16[32,64,128]{2,1,0:T(8,128)(2,1)S(1)} collective-permute-done((bf16[32,64,128]{2,1,0:T(8,128)(2,1)S(1)}, bf16[32,64,128]{2,1,0:T(8,128)(2,1)S(1)}, u32[]{:S(2)}, u32[]{:S(2)}) %collective-permute-start.3) | collective-permute-done | bytes 524320 | tf_op jit(solution)/shard_map/ppermute | solution.py:19
  73.1 5.2 %collective-permute-done.2 = bf16[32,64,128]{2,1,0:T(8,128)(2,1)S(1)} collective-permute-done((bf16[32,64,128]{2,1,0:T(8,128)(2,1)S(1)}, bf16[32,64,128]{2,1,0:T(8,128)(2,1)S(1)}, u32[]{:S(2)}, u32[]{:S(2)}) %collective-permute-start.2) | collective-permute-done | bytes 524320 | tf_op jit(solution)/shard_map/ppermute | solution.py:17
  78.3 1.5 pad_maximum_fusion.1
  79.8 13.3 %gather_fusion.2 = bf16[448,64,128]{2,1,0:T(8,128)(2,1)} fusion(bf16[128,64,128]{2,1,0:T(8,128)(2,1)S(1)} %pad_maximum_fusion.1, s32[1024]{0:T(1024)S(1)} %pad_clamp_fusion.2), kind=kCustom, calls=%fused_computation.1.clone | custom fusion | bytes 14681856 | tf_op jit(solution)/shard_map/jit(_take)/gather | solution.py:33
  93.1 9.2 %bitcast_subtract_fusion.1 = f32[64,64,128]{2,1,0:T(8,128)S(1)} fusion(f32[64,64,128]{2,1,0:T(8,128)} %param.12, f32[64,128,64]{1,2,0:T(8,128)} %fusion.44, bf16[64,7,64,64]{3,2,1,0:T(8,128)(2,1)} %param.15, bf16[64,7,64,128]{3,2,1,0:T(8,128)(2,1)} %bitcast.57, pred[64,7]{1,0:T(8,128)(4,1)S(1)} %copy.17), kind=kOutput, calls=%fused_computation.22 | convolution fusion | flops 474480640 | bytes 17301952 | tf_op jit(solution)/shard_map/njab,njbk->nak/dot_general | solution.py:34
  102.3 3.8 %fusion.14 = f32[64,64,128]{2,0,1:T(8,128)} fusion(f32[64,64,128]{2,1,0:T(8,128)S(1)} %bitcast_subtract_fusion.1, s32[64]{0:T(128)S(1)} %get-tuple-element.7), kind=kOutput, calls=%fused_computation.28 | convolution fusion | flops 402657280 | bytes 4194560 | tf_op jit(solution)/shard_map/fc,fak->cak/dot_general | solution.py:77
  107.1 71.5 %all-reduce.2.cloned.1.call-done = f32[64,64,128]{2,0,1:T(8,128)} async-done(((f32[64,64,128]{2,0,1:T(8,128)}), f32[64,64,128]{2,0,1:T(8,128)}) %all-reduce.2.cloned.1.call-update) | async-done | bytes 2097168 | tf_op jit(solution)/shard_map/psum | solution.py:80
  178.6 1.8 convert_element_type.29
  180.4 2.3 fusion.23
  184.3 4.4 %collective-permute-start.5 = (bf16[32,64,128]{2,1,0:T(8,128)(2,1)}, bf16[32,64,128]{2,1,0:T(8,128)(2,1)}, u32[]{:S(2)}, u32[]{:S(2)}) collective-permute-start(bf16[32,64,128]{2,1,0:T(8,128)(2,1)} %get-tuple-element.13), channel_id=1, source_target_pairs={{1,0},{2,1},{3,2},{4,3},{5,4},{6,5},{7,6},{8,7},{9,8},{10,9},{11,1... | collective-permute-start | bytes 1572872 | tf_op jit(solution)/shard_map/ppermute | solution.py:19
  188.8 1.9 collective-permute-start.4
  190.8 3.1 %fusion.28 = f32[64,128,64]{1,2,0:T(8,128)} fusion(bf16[64,64,64]{2,1,0:T(8,128)(2,1)} %param.18, f32[64,128,64]{1,2,0:T(8,128)S(1)} %fusion.23), kind=kOutput, calls=%fused_computation.40 | convolution fusion | flops 68157440 | bytes 4718592 | tf_op jit(solution)/shard_map/nab,nbk->nak/dot_general | solution.py:27
  193.9 3.5 %collective-permute-done.5 = bf16[32,64,128]{2,1,0:T(8,128)(2,1)} collective-permute-done((bf16[32,64,128]{2,1,0:T(8,128)(2,1)}, bf16[32,64,128]{2,1,0:T(8,128)(2,1)}, u32[]{:S(2)}, u32[]{:S(2)}) %collective-permute-start.5) | collective-permute-done | bytes 524320 | tf_op jit(solution)/shard_map/ppermute | solution.py:19
  197.5 7.4 %collective-permute-done.4 = bf16[32,64,128]{2,1,0:T(8,128)(2,1)} collective-permute-done((bf16[32,64,128]{2,1,0:T(8,128)(2,1)}, bf16[32,64,128]{2,1,0:T(8,128)(2,1)}, u32[]{:S(2)}, u32[]{:S(2)}) %collective-permute-start.4) | collective-permute-done | bytes 524320 | tf_op jit(solution)/shard_map/ppermute | solution.py:17
  206.3 13.3 %gather_fusion.3 = bf16[448,64,128]{2,1,0:T(8,128)(2,1)} fusion(bf16[128,64,128]{2,1,0:T(8,128)(2,1)S(1)} %pad_maximum_fusion.2, s32[1024]{0:T(1024)S(1)} %pad_clamp_fusion.1), kind=kCustom, calls=%fused_computation.2.clone | custom fusion | bytes 14681856 | tf_op jit(solution)/shard_map/jit(_take)/gather | solution.py:33
  219.6 6.8 %fusion = f32[64,128,64,1]{1,2,3,0:T(8,128)S(1)} fusion(bf16[64,7,64,64]{3,2,1,0:T(8,128)(2,1)} %param.20, bf16[64,7,64,128]{3,2,1,0:T(8,128)(2,1)} %bitcast.58, pred[64,7]{1,0:T(8,128)(4,1)S(1)} %copy.23), kind=kOutput, calls=%fused_computation.4 | convolution fusion | flops 473432064 | bytes 13107648 | tf_op jit(solution)/shard_map/njab,njbk->nak/dot_general | solution.py:34
  226.5 2.4 fusion.12
  228.9 2.6 %add_bitcast_fusion = f32[64,64,128]{2,1,0:T(8,128)} fusion(f32[64,128,64]{1,2,0:T(8,128)S(1)} %copy-done.3, bf16[64,64,64]{2,1,0:T(8,128)(2,1)S(1)} %copy-done.10, bf16[64,64,128]{2,0,1:T(8,128)(2,1)S(1)} %fusion.12), kind=kOutput, calls=%fused_computation.31 | convolution fusion | flops 68681728 | bytes 5767168 | tf_op jit(solution)/shard_map/nab,nbk->nak/dot_general | solution.py:27
  231.5 2.3 gather_fusion
  233.8 3.3 %select_add_fusion = f32[64,64,128]{2,1,0:T(8,128)} fusion(f32[64,64,128]{2,1,0:T(8,128)} %get-tuple-element.21, f32[64,64,128]{2,1,0:T(8,128)S(1)} %gather_fusion, pred[64]{0:T(512)(128)(4,1)S(1)} %get-tuple-element.6), kind=kLoop, calls=%fused_computation.30 | loop fusion | flops 1048576 | bytes 6291520 | tf_op jit(solution)/shard_map/add | solution.py:89
  (48 shorter events, 6.9 us)
Async XLA Ops:
  6.5 1.2 copy-start
  6.5 172.0 %all-reduce.2.cloned.1.call-start = ((), (), s32[]{:S(2)}) async-start(), calls=%async_computation | async-start | bytes 4194304 | tf_op jit(solution)/shard_map/psum | solution.py:80
  11.1 9.3 %copy-start.4 = (bf16[64,64,128]{2,1,0:T(8,128)(2,1)}, bf16[64,64,128]{2,1,0:T(8,128)(2,1)S(1)}, u32[]{:S(2)}) copy-start(bf16[64,64,128]{2,1,0:T(8,128)(2,1)S(1)} %get-tuple-element.18) | copy-start | bytes 3145732
  11.1 7.1 %copy-start.11 = (s32[64,7]{0,1:T(8,128)S(1)}, s32[64,7]{0,1:T(8,128)}, u32[]{:S(2)}) copy-start(s32[64,7]{0,1:T(8,128)} %param.16) | copy-start | bytes 5380
  11.1 7.4 %copy-start.8 = (bf16[64,64,64]{2,1,0:T(8,128)(2,1)S(1)}, bf16[64,64,64]{2,1,0:T(8,128)(2,1)}, u32[]{:S(2)}) copy-start(bf16[64,64,64]{2,1,0:T(8,128)(2,1)} %param.13) | copy-start | bytes 1572868
  12.2 15.1 %collective-permute-start.1 = (bf16[32,64,128]{2,1,0:T(8,128)(2,1)}, bf16[32,64,128]{2,1,0:T(8,128)(2,1)}, u32[]{:S(2)}, u32[]{:S(2)}) collective-permute-start(bf16[32,64,128]{2,1,0:T(8,128)(2,1)} %get-tuple-element.17), channel_id=1, source_target_pairs={{1,0},{2,1},{3,2},{4,3},{5,4},{6,5},{7,6},{8,7},{9,8},{10,9},{11,1... | collective-permute-start | bytes 1572872 | tf_op jit(solution)/shard_map/ppermute | solution.py:19
  16.2 18.0 %collective-permute-start = (bf16[32,64,128]{2,1,0:T(8,128)(2,1)}, bf16[32,64,128]{2,1,0:T(8,128)(2,1)}, u32[]{:S(2)}, u32[]{:S(2)}) collective-permute-start(bf16[32,64,128]{2,1,0:T(8,128)(2,1)} %get-tuple-element.16), channel_id=1, source_target_pairs={{0,1},{1,2},{2,3},{3,4},{4,5},{5,6},{6,7},{7,8},{8,9},{9,10},{10,1... | collective-permute-start | bytes 1572872 | tf_op jit(solution)/shard_map/ppermute | solution.py:17
  59.4 7.6 %copy-start.5 = (bf16[64,64,128]{2,1,0:T(8,128)(2,1)}, bf16[64,64,128]{2,1,0:T(8,128)(2,1)S(1)}, u32[]{:S(2)}) copy-start(bf16[64,64,128]{2,1,0:T(8,128)(2,1)S(1)} %get-tuple-element.20) | copy-start | bytes 3145732
  59.4 5.7 %copy-start.13 = (s32[64]{0:T(128)S(1)}, s32[64]{0:T(128)}, u32[]{:S(2)}) copy-start(s32[64]{0:T(128)} %param.17) | copy-start | bytes 772
  59.4 5.7 %copy-start.9 = (bf16[64,64,64]{2,1,0:T(8,128)(2,1)S(1)}, bf16[64,64,64]{2,1,0:T(8,128)(2,1)}, u32[]{:S(2)}) copy-start(bf16[64,64,64]{2,1,0:T(8,128)(2,1)} %param.13) | copy-start | bytes 1572868
  59.5 13.6 %collective-permute-start.3 = (bf16[32,64,128]{2,1,0:T(8,128)(2,1)S(1)}, bf16[32,64,128]{2,1,0:T(8,128)(2,1)S(1)}, u32[]{:S(2)}, u32[]{:S(2)}) collective-permute-start(bf16[32,64,128]{2,1,0:T(8,128)(2,1)S(1)} %get-tuple-element.15), channel_id=1, source_target_pairs={{1,0},{2,1},{3,2},{4,3},{5,4},{6,5},{7,6},{8,7},{9,8},{10,9},{11,1... | collective-permute-start | bytes 1572872 | tf_op jit(solution)/shard_map/ppermute | solution.py:19
  61.6 16.8 %collective-permute-start.2 = (bf16[32,64,128]{2,1,0:T(8,128)(2,1)S(1)}, bf16[32,64,128]{2,1,0:T(8,128)(2,1)S(1)}, u32[]{:S(2)}, u32[]{:S(2)}) collective-permute-start(bf16[32,64,128]{2,1,0:T(8,128)(2,1)S(1)} %get-tuple-element.14), channel_id=1, source_target_pairs={{0,1},{1,2},{2,3},{3,4},{4,5},{5,6},{6,7},{7,8},{8,9},{9,10},{10,1... | collective-permute-start | bytes 1572872 | tf_op jit(solution)/shard_map/ppermute | solution.py:17
  106.1 0.7 copy-start.12
  182.6 8.2 %copy-start.2 = (f32[64,128,64]{1,2,0:T(8,128)}, f32[64,128,64]{1,2,0:T(8,128)S(1)}, u32[]{:S(2)}) copy-start(f32[64,128,64]{1,2,0:T(8,128)S(1)} %fusion.23) | copy-start | bytes 6291460
  184.3 13.1 %collective-permute-start.5 = (bf16[32,64,128]{2,1,0:T(8,128)(2,1)}, bf16[32,64,128]{2,1,0:T(8,128)(2,1)}, u32[]{:S(2)}, u32[]{:S(2)}) collective-permute-start(bf16[32,64,128]{2,1,0:T(8,128)(2,1)} %get-tuple-element.13), channel_id=1, source_target_pairs={{1,0},{2,1},{3,2},{4,3},{5,4},{6,5},{7,6},{8,7},{9,8},{10,9},{11,1... | collective-permute-start | bytes 1572872 | tf_op jit(solution)/shard_map/ppermute | solution.py:19
  188.8 16.1 %collective-permute-start.4 = (bf16[32,64,128]{2,1,0:T(8,128)(2,1)}, bf16[32,64,128]{2,1,0:T(8,128)(2,1)}, u32[]{:S(2)}, u32[]{:S(2)}) collective-permute-start(bf16[32,64,128]{2,1,0:T(8,128)(2,1)} %get-tuple-element.12), channel_id=1, source_target_pairs={{0,1},{1,2},{2,3},{3,4},{4,5},{5,6},{6,7},{7,8},{8,9},{9,10},{10,1... | collective-permute-start | bytes 1572872 | tf_op jit(solution)/shard_map/ppermute | solution.py:17
  219.6 6.9 %copy-start.6 = (f32[64,64,128]{2,0,1:T(8,128)S(1)}, f32[64,64,128]{2,0,1:T(8,128)}, u32[]{:S(2)}) copy-start(f32[64,64,128]{2,0,1:T(8,128)} %all-reduce.2.cloned.1.call-done) | copy-start | bytes 6291460
  219.6 6.9 %copy-start.7 = (f32[64,128,64]{1,2,0:T(8,128)S(1)}, f32[64,128,64]{1,2,0:T(8,128)}, u32[]{:S(2)}) copy-start(f32[64,128,64]{1,2,0:T(8,128)} %fusion.28) | copy-start | bytes 6291460
  226.5 2.4 copy-start.3
  226.5 2.4 copy-start.10
  233.8 3.3 %copy-start.1 = (bf16[64,64,64]{2,1,0:T(8,128)(2,1)S(1)}, bf16[64,64,64]{2,1,0:T(8,128)(2,1)}, u32[]{:S(2)}) copy-start(bf16[64,64,64]{2,1,0:T(8,128)(2,1)} %param.14) | copy-start | bytes 1572868
Sparse Core Ops, SparseCore 0:
  106.3 72.2 all-reduce.1
where the time goes:
time: 248 us; the launch traced here: 244 us
  waiting for transfers between devices  108 us (44%)
  local copies, waits for them, and re-layouts  47.4 us (19%)
  matrix products  44.8 us (18%)
  starting transfers between devices  17.9 us (7%)
  between operations  13.7 us (6%)
  other arithmetic  12.4 us (5%)
    psum x1, waiting for transfers between devices, on_device(): coarse_rhs = lax.psum(partial_sum, 'grp')  71.5 us
    gather x3, local copies, waits for them, and re-layouts, nearby_product(): nearby = jnp.take(extended, columns - first_row, axis=0)  40 us
    dot_general x7, matrix products, block_product(): jnp.einsum('nab,nbk->nak', blocks, vector.astype(jnp.bfloat16), preferred...  25 us
    ppermute x3, waiting for transfers between devices, extended_2(): lax.ppermute(tail, axis, [(i, (i + 1) % count) for i in range(ends)])  19.6 us
    ppermute x3, waiting for transfers between devices, extended_2(): lax.ppermute(head, axis, [((i + 1) % count, i) for i in range(ends)])  16.5 us
    dot_general x2, matrix products, nearby_product(): jnp.einsum('njab,njbk->nak', off_blocks, nearby, preferred_element_type=j...  16 us
    ppermute x3, starting transfers between devices, extended_2(): lax.ppermute(head, axis, [((i + 1) % count, i) for i in range(ends)])  10.5 us
    ppermute x3, starting transfers between devices, extended_2(): lax.ppermute(tail, axis, [(i, (i + 1) % count) for i in range(ends)])  7.39 us
  transfers between devices with their start and end apart: 7, of which 7 were waited for; matrix products, arithmetic and copies ran while one was open for 3% of the time, Pallas kernels for 0%

commit v1 on v0

v1 whole, which is shorter than its diff:
```python
import functools

import jax
import jax.numpy as jnp
from jax import lax
from jax.experimental import pallas as pl
from jax.experimental.pallas import tpu as pltpu
from jax.sharding import PartitionSpec as P

f32, bf16 = jnp.float32, jnp.bfloat16
damping = 0.8
fine_axes = ("grp", "rows")


def dot(a, b):
    return jnp.dot(a, b, preferred_element_type=f32)


def params(mib):
    return pltpu.CompilerParams(vmem_limit_bytes=mib << 20)


def cost(flops, nbytes):
    return pl.CostEstimate(flops=flops, bytes_accessed=nbytes, transcendentals=0)


def row_block(step, *tail):
    return pl.BlockSpec((step,) + tail, lambda i: (i,) + (0,) * len(tail))


vmem = pl.BlockSpec(memory_space=pltpu.VMEM)
smem = pl.BlockSpec(memory_space=pltpu.SMEM)
hbm = pl.BlockSpec(memory_space=pltpu.HBM)


def shape(kind, *dims):
    return jax.ShapeDtypeStruct(dims, kind)


def in_hbm(array):
    return pltpu.with_memory_space_constraint(array, pltpu.HBM)


def first_kernel(step, smoother, rhs, low, high, smoother_here, rhs_here, sem):
    n, half = rhs.shape[0], low.shape[0]
    copies = []
    for s in range(0, n, step):
        rows = slice(s, s + step)
        k = 2 * (s // step)
        pair = (
            pltpu.make_async_copy(smoother.at[rows], smoother_here.at[rows], sem.at[k]),
            pltpu.make_async_copy(rhs.at[rows], rhs_here.at[rows], sem.at[k + 1]),
        )
        for c in pair:
            c.start()
        copies.append(pair)
    for s in range(0, n, step):
        for c in copies[s // step]:
            c.wait()
        products = [dot(smoother_here[r], rhs_here[r].astype(bf16)) for r in range(s, s + step)]
        for r in range(s, s + step):
            out = low if r < half else high
            out[r % half] = (damping * products[r - s]).astype(bf16)


def first_iterate(smoother, rhs):
    n, b, k = rhs.shape
    step = 16
    return pl.pallas_call(
        functools.partial(first_kernel, step),
        in_specs=[hbm, hbm],
        out_specs=[vmem, vmem],
        out_shape=[shape(bf16, n // 2, b, k)] * 2,
        scratch_shapes=[
            pltpu.VMEM((n, b, b), bf16),
            pltpu.VMEM((n, b, k), f32),
            pltpu.SemaphoreType.DMA((2 * n // step,)),
        ],
        compiler_params=params(16),
        cost_estimate=cost(2 * n * b * b * k, 6 * n * b * k + 4 * n * b * b),
        name="first_iterate",
    )(in_hbm(smoother), in_hbm(rhs))


def pack_kernel(step, off, diag, out):
    for r in range(step):
        out[r] = jnp.concatenate([off[r, j] for j in range(off.shape[1])] + [diag[r]], axis=1)


def packed(off, diag):
    rows, near, b, _ = off.shape
    step = 16
    return pl.pallas_call(
        functools.partial(pack_kernel, step),
        grid=(rows // step,),
        in_specs=[row_block(step, near, b, b), row_block(step, b, b)],
        out_specs=row_block(step, b, (near + 1) * b),
        out_shape=shape(bf16, rows, b, (near + 1) * b),
        compiler_params=params(16),
        cost_estimate=cost(0, 6 * rows * b * b * (near + 1)),
        name="packed",
    )(in_hbm(off), in_hbm(diag))


def load_extended(extended, *parts):
    at = 0
    for part in parts:
        extended[at : at + part.shape[0]] = part[...]
        at += part.shape[0]


def images(step, s, cols, base, skip, own, blocks, extended):
    out = []
    for r in range(step):
        i = s * step + r
        vector = [extended[cols[j, skip + i] - base] for j in range(cols.shape[0])]
        vector.append(extended[own + i])
        out.append(dot(blocks[skip + i], jnp.concatenate(vector, axis=0)))
    return out


def fine_start(height):
    return (lax.axis_index("grp") * lax.axis_size("rows") + lax.axis_index("rows")) * height


def kept_side():
    return (lax.axis_index("grp") + lax.axis_index("rows")) & 1


def second_kernel(
    step, upper, cols, first_part, middle, last_part, blocks, smoother, rhs, out, out_low, extended
):
    half = out.shape[0]
    load_extended(extended, first_part, middle, last_part)
    skip = half if upper else 0
    base = fine_start(rhs.shape[0]) + skip - half

    @pl.loop(0, half // step)
    def _(s):
        image = images(step, s, cols, base, skip, half, blocks, extended)
        rows = [s * step + r for r in range(step)]
        right = [rhs[skip + i] for i in rows]
        first = [dot(smoother[skip + i], right[r].astype(bf16)) for r, i in enumerate(rows)]
        residual = [(right[r] - image[r]).astype(bf16) for r in range(step)]
        products = [dot(smoother[skip + i], residual[r]) for r, i in enumerate(rows)]
        for r, i in enumerate(rows):
            second = damping * first[r] + damping * products[r]
            out[i] = second
            out_low[i] = second.astype(bf16)


def second_iterate(upper, cols, parts, blocks, smoother, rhs):
    n, b, k = rhs.shape
    near, half, step = cols.shape[0], n // 2, 16
    return pl.pallas_call(
        functools.partial(second_kernel, step, upper),
        in_specs=[smem] + [vmem] * 6,
        out_specs=[vmem] * 2,
        out_shape=[shape(f32, half, b, k), shape(bf16, half, b, k)],
        scratch_shapes=[pltpu.VMEM((3 * half, b, k), bf16)],
        compiler_params=params(12),
        cost_estimate=cost(n * b * b * k * (near + 3), n * b * b * (near + 2) + 7 * n * b * k),
        name="second_upper" if upper else "second_lower",
    )(cols, *parts, blocks, smoother, rhs)


def restrict_kernel(step, upper, cols, aggregate, first_part, middle, last_part, blocks, rhs, *rest):
    before, (total, extended) = rest[:-2], rest[-2:]
    half, coarse = middle.shape[0], total.shape[0]
    load_extended(extended, first_part, middle, last_part)
    if not before:
        total[...] = jnp.zeros_like(total)
    skip = half if upper else 0
    base = fine_start(rhs.shape[0]) + skip - half
    turn = kept_side() * (coarse // 2) - lax.axis_index("rows") * coarse + coarse

    @pl.loop(0, half // step)
    def _(s):
        image = images(step, s, cols, base, skip, half, blocks, extended)
        residual = [rhs[skip + s * step + r] - image[r] for r in range(step)]
        for r in range(step):
            slot = lax.rem(aggregate[skip + s * step + r] + turn, coarse)
            total[slot] = total[slot] + residual[r]


def restricted(upper, cols, aggregate, parts, blocks, rhs, coarse, *before):
    n, b, k = rhs.shape
    near, half, step = cols.shape[0], n // 2, 16
    return pl.pallas_call(
        functools.partial(restrict_kernel, step, upper),
        in_specs=[smem, smem] + [vmem] * (5 + len(before)),
        out_specs=vmem,
        out_shape=shape(f32, coarse, b, k),
        scratch_shapes=[pltpu.VMEM((3 * half, b, k), bf16)],
        input_output_aliases={7: 0} if before else {},
        compiler_params=params(12),
        cost_estimate=cost(n * b * b * k * (near + 1), n * b * b * (near + 1) + 6 * n * b * k),
        name="restrict_upper" if upper else "restrict_lower",
    )(cols, aggregate, *parts, blocks, rhs, *before)


def coarse_first_kernel(upper, lower, more_upper, more_lower, smoother, rhs, first):
    quarter = upper.shape[0]
    skip = kept_side() * 2 * quarter
    for total, more, at in ((upper, more_upper, 0), (lower, more_lower, quarter)):
        full = [total[r] + more[r].astype(f32) for r in range(quarter)]
        products = [dot(smoother[skip + at + r], full[r].astype(bf16)) for r in range(quarter)]
        for r in range(quarter):
            rhs[at + r] = full[r]
            first[at + r] = (damping * products[r]).astype(bf16)


def coarse_first(upper, lower, more_upper, more_lower, smoother):
    n, b, k = 2 * upper.shape[0], upper.shape[1], upper.shape[2]
    return pl.pallas_call(
        coarse_first_kernel,
        in_specs=[vmem] * 5,
        out_specs=[vmem] * 2,
        out_shape=[shape(f32, n, b, k), shape(bf16, n, b, k)],
        compiler_params=params(16),
        cost_estimate=cost(2 * n * b * b * k, 12 * n * b * k + 4 * n * b * b),
        name="coarse_first",
    )(upper, lower, more_upper, more_lower, smoother)


def coarse_second_kernel(
    step, cols, halo, own, other, blocks, smoother, rhs, out, extended
):
    n = own.shape[0]
    skip = kept_side() * n
    base = lax.axis_index("rows") * 2 * n + skip - n
    at = 2 * skip
    extended[pl.ds(at, n)] = halo[...]
    extended[n : 2 * n] = own[...]
    extended[pl.ds(2 * n - at, n)] = other[...]

    @pl.loop(0, n // step)
    def _(s):
        image = images(step, s, cols, base, skip, n, blocks, extended)
        rows = [s * step + r for r in range(step)]
        first = [damping * dot(smoother[skip + i], rhs[i].astype(bf16)) for i in rows]
        residual = [(rhs[i] - image[r]).astype(bf16) for r, i in enumerate(rows)]
        products = [dot(smoother[skip + i], residual[r]) for r, i in enumerate(rows)]
        for r, i in enumerate(rows):
            out[i] = first[r] + damping * products[r]


def coarse_second(cols, halo, own, other, blocks, smoother, rhs):
    n, b, k = rhs.shape
    near, step = cols.shape[0], 16
    return pl.pallas_call(
        functools.partial(coarse_second_kernel, step),
        in_specs=[smem] + [vmem] * 6,
        out_specs=vmem,
        out_shape=shape(f32, n, b, k),
        scratch_shapes=[pltpu.VMEM((3 * n, b, k), bf16)],
        compiler_params=params(12),
        cost_estimate=cost(2 * n * b * b * k * (near + 3), 2 * n * b * b * (near + 2) + 14 * n * b * k),
        name="coarse_second",
    )(cols, halo, own, other, blocks, smoother, rhs)


def correct_kernel(aggregate, lower, upper, kept, given, out, table, staged, sem):
    half, n = kept.shape[0], staged.shape[0]
    turn = kept_side() * half - lax.axis_index("rows") * 2 * half + 2 * half
    table[0:half] = kept[...]
    table[half : 2 * half] = given[...]
    copies = []
    for s in range(sem.shape[0]):
        step = n // sem.shape[0]
        for r in range(s * step, (s + 1) * step):
            fine = lower[r] if r < n // 2 else upper[r - n // 2]
            staged[r] = fine + table[lax.rem(aggregate[r] + turn, 2 * half)]
        rows = slice(s * step, (s + 1) * step)
        copies.append(pltpu.make_async_copy(staged.at[rows], out.at[rows], sem.at[s]))
        copies[-1].start()
    for c in copies:
        c.wait()


def corrected(aggregate, lower, upper, kept, given):
    n, b, k = aggregate.shape[0], lower.shape[1], lower.shape[2]
    return pl.pallas_call(
        correct_kernel,
        in_specs=[smem] + [vmem] * 4,
        out_specs=hbm,
        out_shape=shape(f32, n, b, k),
        scratch_shapes=[
            pltpu.VMEM((2 * kept.shape[0], b, k), f32),
            pltpu.VMEM((n, b, k), f32),
            pltpu.SemaphoreType.DMA((4,)),
        ],
        compiler_params=params(16),
        cost_estimate=cost(n * b * k, 12 * n * b * k),
        name="corrected",
    )(aggregate, lower, upper, kept, given)


def on_device(
    rhs,
    fine_diag,
    fine_smoother,
    fine_blocks,
    fine_cols,
    aggregate,
    coarse_diag,
    coarse_smoother,
    coarse_blocks,
    coarse_cols,
):
    grp, rows = lax.axis_size("grp"), lax.axis_size("rows")
    coarse = coarse_diag.shape[0]
    half = coarse // 2
    fine_cols, coarse_cols = fine_cols.T, coarse_cols.T
    ends = range(grp * rows - 1)
    to_next = lambda v: lax.ppermute(v, fine_axes, [(i, i + 1) for i in ends])
    to_previous = lambda v: lax.ppermute(v, fine_axes, [(i + 1, i) for i in ends])

    low, high = first_iterate(fine_smoother, rhs)
    before, after = to_next(high), to_previous(low)
    fine = packed(fine_blocks, fine_diag)
    lower, low2 = second_iterate(False, fine_cols, (before, low, high), fine, fine_smoother, rhs)
    after2 = to_previous(low2)
    upper, high2 = second_iterate(True, fine_cols, (low, high, after), fine, fine_smoother, rhs)
    before2 = to_next(high2)
    after2, blocks = lax.optimization_barrier((after2, packed(coarse_blocks, coarse_diag)))
    total = restricted(True, fine_cols, aggregate, (low2, high2, after2), fine, rhs, coarse)
    total = restricted(False, fine_cols, aggregate, (before2, low2, high2), fine, rhs, coarse, total)
    kept, given = total[:half], total[half:]

    across = [(i, i ^ 1) for i in range(grp)]
    near = [(i, i ^ 2) for i in range(grp)]
    far = [(i, i ^ 6) for i in range(grp)]
    total = kept + lax.ppermute(given, "grp", across)
    quarter = half // 2
    one, two = total[:quarter], total[quarter:]
    from_one = lax.ppermute(one.astype(bf16), "grp", near)
    from_two = lax.ppermute(two.astype(bf16), "grp", far)
    one, two = one + from_one.astype(f32), two + from_two.astype(f32)
    from_one = lax.ppermute(one.astype(bf16), "grp", far)
    from_two = lax.ppermute(two.astype(bf16), "grp", near)

    coarse_rhs, rounded_first = coarse_first(one, two, from_one, from_two, coarse_smoother)
    towards = []
    for i in range(grp):
        for r in range(rows):
            source = r - 1 if (i + r) % 2 == 0 else r + 1
            if 0 <= source < rows:
                towards.append((i * rows + source, i * rows + r))
    other = lax.ppermute(rounded_first, "grp", across)
    halo = lax.ppermute(rounded_first, fine_axes, towards)
    mine = coarse_second(
        coarse_cols,
        halo,
        rounded_first,
        other,
        blocks,
        coarse_smoother,
        coarse_rhs,
    )
    theirs = lax.ppermute(mine, "grp", across)
    return corrected(aggregate, lower, upper, mine, theirs)


def solution(mesh):
    in_specs = (
        P(("grp", "rows"), None, None),
        P(("grp", "rows"), None, None),
        P(("grp", "rows"), None, None),
        P(("grp", "rows"), None, None, None),
        P(("grp", "rows"), None),
        P(("grp", "rows")),
        P("rows", None, None),
        P("rows", None, None),
        P("rows", None, None, None),
        P("rows", None),
    )
    out_specs = P(("grp", "rows"), None, None)
    return jax.shard_map(
        on_device, mesh=mesh, in_specs=in_specs, out_specs=out_specs, check_vma=False
    )
```

time: 248 us -> 94.1 us (0.38)
  the two profiles are of different devices: /device:TPU:129 before, /device:TPU:1 now
where the time goes in v1:
time: 94.1 us; the launch traced here: 93.9 us
  waiting for transfers between devices  41.7 us (44%)
  starting transfers between devices  28.2 us (30%)
  Pallas kernels  23.2 us (25%)
    ppermute x2, waiting for transfers between devices, on_device(): to_next = lambda v: lax.ppermute(v, fine_axes, [(i, i + 1) for i in ends])  15.1 us
    ppermute x2, starting transfers between devices, on_device(): lax.ppermute(v, fine_axes, [(i + 1, i) for i in ends])  13.2 us
    pallas_call x2, Pallas kernels, packed(): pl.pallas_call(functools.partial(pack_kernel, step), grid=(rows // step,)...  8.98 us
    ppermute x1, waiting for transfers between devices, on_device(): halo = lax.ppermute(rounded_first, fine_axes, towards)  7.99 us
    ppermute x1, waiting for transfers between devices, on_device(): from_two = lax.ppermute(two.astype(bf16), 'grp', far)  6.39 us
    ppermute x2, starting transfers between devices, on_device(): to_next = lambda v: lax.ppermute(v, fine_axes, [(i, i + 1) for i in ends])  5.87 us
    ppermute x1, waiting for transfers between devices, on_device(): from_two = lax.ppermute(two.astype(bf16), 'grp', near)  4.64 us
    pallas_call x2, Pallas kernels, second_iterate(): pl.pallas_call(functools.partial(second_kernel, step, upper), in_specs=[s...  4.08 us
  transfers between devices with their start and end apart: 12, of which 9 were waited for; matrix products, arithmetic and copies ran while one was open for 0% of the time, Pallas kernels for 16%

profile of v1, /device:TPU:1, one launch (start us, length us, event | category | flops | bytes accessed | tf_op | source)
XLA Modules:
  0.0 93.9 jit_solution(2451720731712421685)
XLA Ops:
  0.0 2.1 %first_iterate.1 = (bf16[32,64,128]{2,1,0:T(8,128)(2,1)S(1)}, bf16[32,64,128]{2,1,0:T(8,128)(2,1)S(1)}) custom-call(bf16[64,64,64]{2,1,0:T(8,128)(2,1)} %smoother.7, f32[64,64,128]{2,1,0:T(8,128)} %rhs.9), custom_call_target="tpu_custom_call" | custom-call | flops 67108864 | bytes 4194304 | tf_op jit(solution)/shard_map/first_iterate/pallas_call | solution.py:69
  2.1 3.9 %collective-permute-start = (bf16[32,64,128]{2,1,0:T(8,128)(2,1)S(1)}, bf16[32,64,128]{2,1,0:T(8,128)(2,1)S(1)}, u32[]{:S(2)}, u32[]{:S(2)}) collective-permute-start(bf16[32,64,128]{2,1,0:T(8,128)(2,1)S(1)} %get-tuple-element.15.last_part.middle), channel_id=1, source_target_pairs={{0,1},{1,2},{2,3},{3,4},{4,5},{5,6},{6,7},{7,8},{8,9},{9,10},{10,1... | collective-permute-start | bytes 1572872 | tf_op jit(solution)/shard_map/ppermute | solution.py:316
  6.1 9.3 %collective-permute-start.1 = (bf16[32,64,128]{2,1,0:T(8,128)(2,1)S(1)}, bf16[32,64,128]{2,1,0:T(8,128)(2,1)S(1)}, u32[]{:S(2)}, u32[]{:S(2)}) collective-permute-start(bf16[32,64,128]{2,1,0:T(8,128)(2,1)S(1)} %get-tuple-element.16.middle.first_part), channel_id=1, source_target_pairs={{1,0},{2,1},{3,2},{4,3},{5,4},{6,5},{7,6},{8,7},{9,8},{10,9},{11,1... | collective-permute-start | bytes 1572872 | tf_op jit(solution)/shard_map/ppermute | solution.py:317
  15.4 4.5 %packed.2.blocks = bf16[64,64,512]{2,1,0:T(8,128)(2,1)S(1)} custom-call(bf16[64,7,64,64]{3,2,1,0:T(8,128)(2,1)} %off.2, bf16[64,64,64]{2,1,0:T(8,128)(2,1)} %diag.2), custom_call_target="tpu_custom_call" | custom-call | bytes 12582912 | tf_op jit(solution)/shard_map/packed/pallas_call | solution.py:93
  19.9 4.9 %collective-permute-done.first_part = bf16[32,64,128]{2,1,0:T(8,128)(2,1)S(1)} collective-permute-done((bf16[32,64,128]{2,1,0:T(8,128)(2,1)S(1)}, bf16[32,64,128]{2,1,0:T(8,128)(2,1)S(1)}, u32[]{:S(2)}, u32[]{:S(2)}) %collective-permute-start) | collective-permute-done | bytes 524320 | tf_op jit(solution)/shard_map/ppermute | solution.py:316
  24.8 2.0 %second_lower.1 = (f32[32,64,128]{2,1,0:T(8,128)S(1)}, bf16[32,64,128]{2,1,0:T(8,128)(2,1)S(1)}) custom-call(s32[7,64]{1,0:T(8,128)S(1)} %bitcast.2, bf16[32,64,128]{2,1,0:T(8,128)(2,1)S(1)} %collective-permute-done.first_part, bf16[32,64,128]{2,1,0:T(8,128)(2,1)S(1)} %get-tuple-element.16.middle.first_part, ...), custom_call_target="tpu_custom_call" | custom-call | flops 335544320 | bytes 6029312 | tf_op jit(solution)/shard_map/second_lower/pallas_call | solution.py:155
  26.9 3.9 %collective-permute-start.3 = (bf16[32,64,128]{2,1,0:T(8,128)(2,1)S(1)}, bf16[32,64,128]{2,1,0:T(8,128)(2,1)S(1)}, u32[]{:S(2)}, u32[]{:S(2)}) collective-permute-start(bf16[32,64,128]{2,1,0:T(8,128)(2,1)S(1)} %get-tuple-element.20.first_part.middle), channel_id=1, source_target_pairs={{1,0},{2,1},{3,2},{4,3},{5,4},{6,5},{7,6},{8,7},{9,8},{10,9},{11,1... | collective-permute-start | bytes 1572872 | tf_op jit(solution)/shard_map/ppermute | solution.py:317
  30.8 2.0 %second_upper.1 = (f32[32,64,128]{2,1,0:T(8,128)S(1)}, bf16[32,64,128]{2,1,0:T(8,128)(2,1)S(1)}) custom-call(s32[7,64]{1,0:T(8,128)S(1)} %bitcast.3, bf16[32,64,128]{2,1,0:T(8,128)(2,1)S(1)} %get-tuple-element.16.middle.first_part, bf16[32,64,128]{2,1,0:T(8,128)(2,1)S(1)} %get-tuple-element.15.last_part.middle, ...), custom_call_target="tpu_custom_call" | custom-call | flops 335544320 | bytes 6029312 | tf_op jit(solution)/shard_map/second_upper/pallas_call | solution.py:155
  32.9 1.9 %collective-permute-start.2 = (bf16[32,64,128]{2,1,0:T(8,128)(2,1)S(1)}, bf16[32,64,128]{2,1,0:T(8,128)(2,1)S(1)}, u32[]{:S(2)}, u32[]{:S(2)}) collective-permute-start(bf16[32,64,128]{2,1,0:T(8,128)(2,1)S(1)} %get-tuple-element.19.middle.last_part), channel_id=1, source_target_pairs={{0,1},{1,2},{2,3},{3,4},{4,5},{5,6},{6,7},{7,8},{8,9},{9,10},{10,1... | collective-permute-start | bytes 1572872 | tf_op jit(solution)/shard_map/ppermute | solution.py:316
  34.8 4.5 %packed.3.blocks = bf16[64,64,512]{2,1,0:T(8,128)(2,1)S(1)} custom-call(bf16[64,7,64,64]{3,2,1,0:T(8,128)(2,1)} %off.3, bf16[64,64,64]{2,1,0:T(8,128)(2,1)} %diag.3), custom_call_target="tpu_custom_call" | custom-call | bytes 12582912 | tf_op jit(solution)/shard_map/packed/pallas_call | solution.py:93
  39.3 1.9 %restrict_upper.1.rest_0_ = f32[64,64,128]{2,1,0:T(8,128)S(1)} custom-call(s32[7,64]{1,0:T(8,128)S(1)} %bitcast.4, s32[64]{0:T(128)S(1)} %copy-done.4, bf16[32,64,128]{2,1,0:T(8,128)(2,1)S(1)} %get-tuple-element.20.first_part.middle, bf16[32,64,128]{2,1,0:T(8,128)(2,1)S(1)} %get-tuple-element.19.middle.last_part, ...), custom_call_target="tpu_custom_call" | custom-call | flops 268435456 | bytes 5242880 | tf_op jit(solution)/shard_map/restrict_upper/pallas_call | solution.py:189
  41.2 10.3 %collective-permute-done.2.first_part = bf16[32,64,128]{2,1,0:T(8,128)(2,1)S(1)} collective-permute-done((bf16[32,64,128]{2,1,0:T(8,128)(2,1)S(1)}, bf16[32,64,128]{2,1,0:T(8,128)(2,1)S(1)}, u32[]{:S(2)}, u32[]{:S(2)}) %collective-permute-start.2) | collective-permute-done | bytes 524320 | tf_op jit(solution)/shard_map/ppermute | solution.py:316
  51.5 1.7 %restrict_lower.1 = f32[64,64,128]{2,1,0:T(8,128)S(1)} custom-call(s32[7,64]{1,0:T(8,128)S(1)} %bitcast.5, s32[64]{0:T(128)S(1)} %copy-done.4, bf16[32,64,128]{2,1,0:T(8,128)(2,1)S(1)} %collective-permute-done.2.first_part, bf16[32,64,128]{2,1,0:T(8,128)(2,1)S(1)} %get-tuple-element.20.first_part.middle, ...), custom_call_target="tpu_custom_call", output_to_operand_aliasing={{}: (7, {})} | custom-call | flops 268435456 | bytes 5242880 | tf_op jit(solution)/shard_map/restrict_lower/pallas_call | solution.py:189
  53.4 2.6 %collective-permute-done.4 = f32[32,64,128]{2,1,0:T(8,128)S(1)} collective-permute-done((f32[32,64,128]{2,1,0:T(8,128)S(1)}, f32[32,64,128]{2,1,0:T(8,128)S(1)}, u32[]{:S(2)}, u32[]{:S(2)}) %collective-permute-start.4) | collective-permute-done | bytes 1048608 | tf_op jit(solution)/shard_map/ppermute | solution.py:334
  56.1 0.1 slice_add_fusion
  56.3 2.5 %collective-permute-start.6 = (bf16[16,64,128]{2,1,0:T(8,128)(2,1)S(1)}, bf16[16,64,128]{2,1,0:T(8,128)(2,1)S(1)}, u32[]{:S(2)}, u32[]{:S(2)}) collective-permute-start(bf16[16,64,128]{2,1,0:T(8,128)(2,1)S(1)} %get-tuple-element.31), channel_id=1, source_target_pairs={{0,192},{32,224},{64,128},{96,160},{128,64},{160,96},{192,0},{224,... | collective-permute-start | bytes 786440 | tf_op jit(solution)/shard_map/ppermute | solution.py:338
  58.8 0.2 collective-permute-start.5
  59.0 6.4 %collective-permute-done.6 = bf16[16,64,128]{2,1,0:T(8,128)(2,1)S(1)} collective-permute-done((bf16[16,64,128]{2,1,0:T(8,128)(2,1)S(1)}, bf16[16,64,128]{2,1,0:T(8,128)(2,1)S(1)}, u32[]{:S(2)}, u32[]{:S(2)}) %collective-permute-start.6) | collective-permute-done | bytes 262176 | tf_op jit(solution)/shard_map/ppermute | solution.py:338
  65.4 0.6 collective-permute-done.5
  66.0 0.2 fusion
  66.2 0.5 collective-permute-start.8
  66.8 1.2 %collective-permute-start.7 = (bf16[16,64,128]{2,1,0:T(8,128)(2,1)S(1)}, bf16[16,64,128]{2,1,0:T(8,128)(2,1)S(1)}, u32[]{:S(2)}, u32[]{:S(2)}) collective-permute-start(bf16[16,64,128]{2,1,0:T(8,128)(2,1)S(1)} %get-tuple-element.29), channel_id=1, source_target_pairs={{0,192},{32,224},{64,128},{96,160},{128,64},{160,96},{192,0},{224,... | collective-permute-start | bytes 786440 | tf_op jit(solution)/shard_map/ppermute | solution.py:340
  68.0 4.6 %collective-permute-done.8.more_lower = bf16[16,64,128]{2,1,0:T(8,128)(2,1)S(1)} collective-permute-done((bf16[16,64,128]{2,1,0:T(8,128)(2,1)S(1)}, bf16[16,64,128]{2,1,0:T(8,128)(2,1)S(1)}, u32[]{:S(2)}, u32[]{:S(2)}) %collective-permute-start.8) | collective-permute-done | bytes 262176 | tf_op jit(solution)/shard_map/ppermute | solution.py:341
  72.6 1.6 %collective-permute-done.7.more_upper = bf16[16,64,128]{2,1,0:T(8,128)(2,1)S(1)} collective-permute-done((bf16[16,64,128]{2,1,0:T(8,128)(2,1)S(1)}, bf16[16,64,128]{2,1,0:T(8,128)(2,1)S(1)}, u32[]{:S(2)}, u32[]{:S(2)}) %collective-permute-start.7) | collective-permute-done | bytes 262176 | tf_op jit(solution)/shard_map/ppermute | solution.py:340
  74.2 0.3 coarse_first.1
  74.5 2.6 %collective-permute-start.10 = (bf16[32,64,128]{2,1,0:T(8,128)(2,1)S(1)}, bf16[32,64,128]{2,1,0:T(8,128)(2,1)S(1)}, u32[]{:S(2)}, u32[]{:S(2)}) collective-permute-start(bf16[32,64,128]{2,1,0:T(8,128)(2,1)S(1)} %get-tuple-element.22.own), channel_id=1, source_target_pairs={{0,32},{32,0},{64,96},{96,64},{128,160},{160,128},{192,224},{224,1... | collective-permute-start | bytes 1572872 | tf_op jit(solution)/shard_map/ppermute | solution.py:350
  77.1 1.9 %collective-permute-start.9 = (bf16[32,64,128]{2,1,0:T(8,128)(2,1)S(1)}, bf16[32,64,128]{2,1,0:T(8,128)(2,1)S(1)}, u32[]{:S(2)}, u32[]{:S(2)}) collective-permute-start(bf16[32,64,128]{2,1,0:T(8,128)(2,1)S(1)} %get-tuple-element.22.own), channel_id=1, source_target_pairs={{2,1},{1,2},{4,3},{3,4},{6,5},{5,6},{8,7},{7,8},{10,9},{9,10},{12,... | collective-permute-start | bytes 1572872 | tf_op jit(solution)/shard_map/ppermute | solution.py:351
  79.0 8.0 %collective-permute-done.9.halo = bf16[32,64,128]{2,1,0:T(8,128)(2,1)S(1)} collective-permute-done((bf16[32,64,128]{2,1,0:T(8,128)(2,1)S(1)}, bf16[32,64,128]{2,1,0:T(8,128)(2,1)S(1)}, u32[]{:S(2)}, u32[]{:S(2)}) %collective-permute-start.9) | collective-permute-done | bytes 524320 | tf_op jit(solution)/shard_map/ppermute | solution.py:351
  87.0 2.0 %coarse_second.1.kept = f32[32,64,128]{2,1,0:T(8,128)S(1)} custom-call(s32[7,64]{1,0:T(8,128)S(1)} %bitcast.6, bf16[32,64,128]{2,1,0:T(8,128)(2,1)S(1)} %collective-permute-done.9.halo, bf16[32,64,128]{2,1,0:T(8,128)(2,1)S(1)} %get-tuple-element.22.own, bf16[32,64,128]{2,1,0:T(8,128)(2,1)S(1)} %collective-permute-done.10.other, ...), custom_call_target="tpu_custom_call" | custom-call | flops 335544320 | bytes 6029312 | tf_op jit(solution)/shard_map/coarse_second/pallas_call | solution.py:251
  89.0 0.1 collective-permute-start.11
  89.1 2.6 %collective-permute-done.11.given = f32[32,64,128]{2,1,0:T(8,128)S(1)} collective-permute-done((f32[32,64,128]{2,1,0:T(8,128)S(1)}, f32[32,64,128]{2,1,0:T(8,128)S(1)}, u32[]{:S(2)}, u32[]{:S(2)}) %collective-permute-start.11) | collective-permute-done | bytes 1048608 | tf_op jit(solution)/shard_map/ppermute | solution.py:361
  91.8 2.1 %corrected.1 = f32[64,64,128]{2,1,0:T(8,128)} custom-call(s32[64]{0:T(128)S(1)} %copy-done.4, f32[32,64,128]{2,1,0:T(8,128)S(1)} %get-tuple-element.17.lower, f32[32,64,128]{2,1,0:T(8,128)S(1)} %get-tuple-element.18.upper, f32[32,64,128]{2,1,0:T(8,128)S(1)} %coarse_second.1.kept, f32[32,64,128]{2,1,0:T(8,128)S(1)} %collective-permute-done.11.given), custom_call_target="tpu_custom_call" | custom-call | flops 524288 | bytes 6291456 | tf_op jit(solution)/shard_map/corrected/pallas_call | solution.py:283
  (18 shorter events, 0.3 us)
Async XLA Ops:
  2.1 22.7 %collective-permute-start = (bf16[32,64,128]{2,1,0:T(8,128)(2,1)S(1)}, bf16[32,64,128]{2,1,0:T(8,128)(2,1)S(1)}, u32[]{:S(2)}, u32[]{:S(2)}) collective-permute-start(bf16[32,64,128]{2,1,0:T(8,128)(2,1)S(1)} %get-tuple-element.15.last_part.middle), channel_id=1, source_target_pairs={{0,1},{1,2},{2,3},{3,4},{4,5},{5,6},{6,7},{7,8},{8,9},{9,10},{10,1... | collective-permute-start | bytes 1572872 | tf_op jit(solution)/shard_map/ppermute | solution.py:316
  6.1 18.7 %copy-start = (f32[64,64,128]{2,1,0:T(8,128)S(1)}, f32[64,64,128]{2,1,0:T(8,128)}, u32[]{:S(2)}) copy-start(f32[64,64,128]{2,1,0:T(8,128)} %rhs.9) | copy-start | bytes 6291460
  6.1 18.7 %copy-start.1 = (bf16[64,64,64]{2,1,0:T(8,128)(2,1)S(1)}, bf16[64,64,64]{2,1,0:T(8,128)(2,1)}, u32[]{:S(2)}) copy-start(bf16[64,64,64]{2,1,0:T(8,128)(2,1)} %smoother.7) | copy-start | bytes 1572868
  6.1 18.7 %copy-start.3 = (s32[64,7]{0,1:T(8,128)S(1)}, s32[64,7]{0,1:T(8,128)}, u32[]{:S(2)}) copy-start(s32[64,7]{0,1:T(8,128)} %param.14) | copy-start | bytes 5380
  6.1 24.7 %collective-permute-start.1 = (bf16[32,64,128]{2,1,0:T(8,128)(2,1)S(1)}, bf16[32,64,128]{2,1,0:T(8,128)(2,1)S(1)}, u32[]{:S(2)}, u32[]{:S(2)}) collective-permute-start(bf16[32,64,128]{2,1,0:T(8,128)(2,1)S(1)} %get-tuple-element.16.middle.first_part), channel_id=1, source_target_pairs={{1,0},{2,1},{3,2},{4,3},{5,4},{6,5},{7,6},{8,7},{9,8},{10,9},{11,1... | collective-permute-start | bytes 1572872 | tf_op jit(solution)/shard_map/ppermute | solution.py:317
  26.9 12.4 %collective-permute-start.3 = (bf16[32,64,128]{2,1,0:T(8,128)(2,1)S(1)}, bf16[32,64,128]{2,1,0:T(8,128)(2,1)S(1)}, u32[]{:S(2)}, u32[]{:S(2)}) collective-permute-start(bf16[32,64,128]{2,1,0:T(8,128)(2,1)S(1)} %get-tuple-element.20.first_part.middle), channel_id=1, source_target_pairs={{1,0},{2,1},{3,2},{4,3},{5,4},{6,5},{7,6},{8,7},{9,8},{10,9},{11,1... | collective-permute-start | bytes 1572872 | tf_op jit(solution)/shard_map/ppermute | solution.py:317
  32.9 6.5 %copy-start.4 = (s32[64]{0:T(128)S(1)}, s32[64]{0:T(128)}, u32[]{:S(2)}) copy-start(s32[64]{0:T(128)} %aggregate.5) | copy-start | bytes 772
  32.9 18.6 %collective-permute-start.2 = (bf16[32,64,128]{2,1,0:T(8,128)(2,1)S(1)}, bf16[32,64,128]{2,1,0:T(8,128)(2,1)S(1)}, u32[]{:S(2)}, u32[]{:S(2)}) collective-permute-start(bf16[32,64,128]{2,1,0:T(8,128)(2,1)S(1)} %get-tuple-element.19.middle.last_part), channel_id=1, source_target_pairs={{0,1},{1,2},{2,3},{3,4},{4,5},{5,6},{6,7},{7,8},{8,9},{9,10},{10,1... | collective-permute-start | bytes 1572872 | tf_op jit(solution)/shard_map/ppermute | solution.py:316
  53.3 2.7 %collective-permute-start.4 = (f32[32,64,128]{2,1,0:T(8,128)S(1)}, f32[32,64,128]{2,1,0:T(8,128)S(1)}, u32[]{:S(2)}, u32[]{:S(2)}) collective-permute-start(f32[32,64,128]{2,1,0:T(8,128)S(1)} %slice.17), channel_id=1, source_target_pairs={{0,32},{32,0},{64,96},{96,64},{128,160},{160,128},{192,224},{224,1... | collective-permute-start | bytes 3145736 | tf_op jit(solution)/shard_map/ppermute | solution.py:334
  56.2 18.0 %copy-start.2 = (bf16[64,64,64]{2,1,0:T(8,128)(2,1)S(1)}, bf16[64,64,64]{2,1,0:T(8,128)(2,1)}, u32[]{:S(2)}) copy-start(bf16[64,64,64]{2,1,0:T(8,128)(2,1)} %smoother.9) | copy-start | bytes 1572868
  56.3 9.1 %collective-permute-start.6 = (bf16[16,64,128]{2,1,0:T(8,128)(2,1)S(1)}, bf16[16,64,128]{2,1,0:T(8,128)(2,1)S(1)}, u32[]{:S(2)}, u32[]{:S(2)}) collective-permute-start(bf16[16,64,128]{2,1,0:T(8,128)(2,1)S(1)} %get-tuple-element.31), channel_id=1, source_target_pairs={{0,192},{32,224},{64,128},{96,160},{128,64},{160,96},{192,0},{224,... | collective-permute-start | bytes 786440 | tf_op jit(solution)/shard_map/ppermute | solution.py:338
  58.8 7.2 %collective-permute-start.5 = (bf16[16,64,128]{2,1,0:T(8,128)(2,1)S(1)}, bf16[16,64,128]{2,1,0:T(8,128)(2,1)S(1)}, u32[]{:S(2)}, u32[]{:S(2)}) collective-permute-start(bf16[16,64,128]{2,1,0:T(8,128)(2,1)S(1)} %get-tuple-element.32), channel_id=1, source_target_pairs={{0,64},{32,96},{64,0},{96,32},{128,192},{160,224},{192,128},{224,1... | collective-permute-start | bytes 786440 | tf_op jit(solution)/shard_map/ppermute | solution.py:337
  66.2 20.8 %copy-start.5 = (s32[64,7]{0,1:T(8,128)S(1)}, s32[64,7]{0,1:T(8,128)}, u32[]{:S(2)}) copy-start(s32[64,7]{0,1:T(8,128)} %param.19) | copy-start | bytes 5380
  66.2 6.4 %collective-permute-start.8 = (bf16[16,64,128]{2,1,0:T(8,128)(2,1)S(1)}, bf16[16,64,128]{2,1,0:T(8,128)(2,1)S(1)}, u32[]{:S(2)}, u32[]{:S(2)}) collective-permute-start(bf16[16,64,128]{2,1,0:T(8,128)(2,1)S(1)} %get-tuple-element.25), channel_id=1, source_target_pairs={{0,64},{32,96},{64,0},{96,32},{128,192},{160,224},{192,128},{224,1... | collective-permute-start | bytes 786440 | tf_op jit(solution)/shard_map/ppermute | solution.py:341
  66.8 7.5 %collective-permute-start.7 = (bf16[16,64,128]{2,1,0:T(8,128)(2,1)S(1)}, bf16[16,64,128]{2,1,0:T(8,128)(2,1)S(1)}, u32[]{:S(2)}, u32[]{:S(2)}) collective-permute-start(bf16[16,64,128]{2,1,0:T(8,128)(2,1)S(1)} %get-tuple-element.29), channel_id=1, source_target_pairs={{0,192},{32,224},{64,128},{96,160},{128,64},{160,96},{192,0},{224,... | collective-permute-start | bytes 786440 | tf_op jit(solution)/shard_map/ppermute | solution.py:340
  74.5 4.5 %collective-permute-start.10 = (bf16[32,64,128]{2,1,0:T(8,128)(2,1)S(1)}, bf16[32,64,128]{2,1,0:T(8,128)(2,1)S(1)}, u32[]{:S(2)}, u32[]{:S(2)}) collective-permute-start(bf16[32,64,128]{2,1,0:T(8,128)(2,1)S(1)} %get-tuple-element.22.own), channel_id=1, source_target_pairs={{0,32},{32,0},{64,96},{96,64},{128,160},{160,128},{192,224},{224,1... | collective-permute-start | bytes 1572872 | tf_op jit(solution)/shard_map/ppermute | solution.py:350
  77.1 9.9 %collective-permute-start.9 = (bf16[32,64,128]{2,1,0:T(8,128)(2,1)S(1)}, bf16[32,64,128]{2,1,0:T(8,128)(2,1)S(1)}, u32[]{:S(2)}, u32[]{:S(2)}) collective-permute-start(bf16[32,64,128]{2,1,0:T(8,128)(2,1)S(1)} %get-tuple-element.22.own), channel_id=1, source_target_pairs={{2,1},{1,2},{4,3},{3,4},{6,5},{5,6},{8,7},{7,8},{10,9},{9,10},{12,... | collective-permute-start | bytes 1572872 | tf_op jit(solution)/shard_map/ppermute | solution.py:351
  89.0 2.7 %collective-permute-start.11 = (f32[32,64,128]{2,1,0:T(8,128)S(1)}, f32[32,64,128]{2,1,0:T(8,128)S(1)}, u32[]{:S(2)}, u32[]{:S(2)}) collective-permute-start(f32[32,64,128]{2,1,0:T(8,128)S(1)} %coarse_second.1.kept), channel_id=1, source_target_pairs={{0,32},{32,0},{64,96},{96,64},{128,160},{160,128},{192,224},{224,1... | collective-permute-start | bytes 3145736 | tf_op jit(solution)/shard_map/ppermute | solution.py:361

commit v2 on v1

--- a/solution.py
+++ b/solution.py
@@ -260,17 +260,17 @@
     )(cols, halo, own, other, blocks, smoother, rhs)
 
 
-def correct_kernel(aggregate, lower, upper, kept, given, out, table, staged, sem):
+def correct_kernel(aggregate, lower, upper, kept, given, out, staged, sem):
     half, n = kept.shape[0], staged.shape[0]
     turn = kept_side() * half - lax.axis_index("rows") * 2 * half + 2 * half
-    table[0:half] = kept[...]
-    table[half : 2 * half] = given[...]
     copies = []
     for s in range(sem.shape[0]):
         step = n // sem.shape[0]
         for r in range(s * step, (s + 1) * step):
             fine = lower[r] if r < n // 2 else upper[r - n // 2]
-            staged[r] = fine + table[lax.rem(aggregate[r] + turn, 2 * half)]
+            slot = lax.rem(aggregate[r] + turn, 2 * half)
+            row = lax.rem(slot, half)
+            staged[r] = fine + jnp.where(slot < half, kept[row], given[row])
         rows = slice(s * step, (s + 1) * step)
         copies.append(pltpu.make_async_copy(staged.at[rows], out.at[rows], sem.at[s]))
         copies[-1].start()
@@ -286,7 +286,6 @@
         out_specs=hbm,
         out_shape=shape(f32, n, b, k),
         scratch_shapes=[
-            pltpu.VMEM((2 * kept.shape[0], b, k), f32),
             pltpu.VMEM((n, b, k), f32),
             pltpu.SemaphoreType.DMA((4,)),
         ],
@@ -323,7 +322,6 @@
     after2 = to_previous(low2)
     upper, high2 = second_iterate(True, fine_cols, (low, high, after), fine, fine_smoother, rhs)
     before2 = to_next(high2)
-    after2, blocks = lax.optimization_barrier((after2, packed(coarse_blocks, coarse_diag)))
     total = restricted(True, fine_cols, aggregate, (low2, high2, after2), fine, rhs, coarse)
     total = restricted(False, fine_cols, aggregate, (before2, low2, high2), fine, rhs, coarse, total)
     kept, given = total[:half], total[half:]
@@ -347,8 +345,9 @@
             source = r - 1 if (i + r) % 2 == 0 else r + 1
             if 0 <= source < rows:
                 towards.append((i * rows + source, i * rows + r))
-    other = lax.ppermute(rounded_first, "grp", across)
     halo = lax.ppermute(rounded_first, fine_axes, towards)
+    own, blocks = lax.optimization_barrier((rounded_first, packed(coarse_blocks, coarse_diag)))
+    other = lax.ppermute(own, "grp", across)
     mine = coarse_second(
         coarse_cols,
         halo,

time: 94.1 us -> 92 us (0.978)
  the two profiles are of different devices: /device:TPU:1 before, /device:TPU:129 now
where the time goes in v2:
time: 92 us; the launch traced here: 91.8 us
  waiting for transfers between devices  34.9 us (38%)
  starting transfers between devices  33 us (36%)
  Pallas kernels  23.1 us (25%)
    ppermute x2, waiting for transfers between devices, on_device(): to_next = lambda v: lax.ppermute(v, fine_axes, [(i, i + 1) for i in ends])  9.99 us
    pallas_call x2, Pallas kernels, packed(): pl.pallas_call(functools.partial(pack_kernel, step), grid=(rows // step,)...  8.97 us
    ppermute x2, starting transfers between devices, on_device(): lax.ppermute(v, fine_axes, [(i + 1, i) for i in ends])  7.67 us
    ppermute x1, starting transfers between devices, on_device(): theirs = lax.ppermute(mine, 'grp', across)  7.12 us
    ppermute x2, starting transfers between devices, on_device(): to_next = lambda v: lax.ppermute(v, fine_axes, [(i, i + 1) for i in ends])  6.48 us
    ppermute x2, waiting for transfers between devices, on_device(): lax.ppermute(v, fine_axes, [(i + 1, i) for i in ends])  6.41 us
    ppermute x1, waiting for transfers between devices, on_device(): from_two = lax.ppermute(two.astype(bf16), 'grp', far)  6.13 us
    ppermute x1, waiting for transfers between devices, on_device(): halo = lax.ppermute(rounded_first, fine_axes, towards)  5.35 us
  transfers between devices with their start and end apart: 12, of which 10 were waited for; matrix products, arithmetic and copies ran while one was open for 0% of the time, Pallas kernels for 16%

profile of v2, /device:TPU:129, one launch (start us, length us, event | category | flops | bytes accessed | tf_op | source)
XLA Modules:
  0.0 91.8 jit_solution(10485653532680211656)
XLA Ops:
  0.0 2.1 %first_iterate.1 = (bf16[32,64,128]{2,1,0:T(8,128)(2,1)S(1)}, bf16[32,64,128]{2,1,0:T(8,128)(2,1)S(1)}) custom-call(bf16[64,64,64]{2,1,0:T(8,128)(2,1)} %smoother.7, f32[64,64,128]{2,1,0:T(8,128)} %rhs.9), custom_call_target="tpu_custom_call" | custom-call | flops 67108864 | bytes 4194304 | tf_op jit(solution)/shard_map/first_iterate/pallas_call | solution.py:69
  2.1 3.1 %collective-permute-start = (bf16[32,64,128]{2,1,0:T(8,128)(2,1)S(1)}, bf16[32,64,128]{2,1,0:T(8,128)(2,1)S(1)}, u32[]{:S(2)}, u32[]{:S(2)}) collective-permute-start(bf16[32,64,128]{2,1,0:T(8,128)(2,1)S(1)} %get-tuple-element.15.last_part.middle), channel_id=1, source_target_pairs={{0,1},{1,2},{2,3},{3,4},{4,5},{5,6},{6,7},{7,8},{8,9},{9,10},{10,1... | collective-permute-start | bytes 1572872 | tf_op jit(solution)/shard_map/ppermute | solution.py:315
  5.3 5.7 %collective-permute-start.1 = (bf16[32,64,128]{2,1,0:T(8,128)(2,1)S(1)}, bf16[32,64,128]{2,1,0:T(8,128)(2,1)S(1)}, u32[]{:S(2)}, u32[]{:S(2)}) collective-permute-start(bf16[32,64,128]{2,1,0:T(8,128)(2,1)S(1)} %get-tuple-element.16.middle.first_part), channel_id=1, source_target_pairs={{1,0},{2,1},{3,2},{4,3},{5,4},{6,5},{7,6},{8,7},{9,8},{10,9},{11,1... | collective-permute-start | bytes 1572872 | tf_op jit(solution)/shard_map/ppermute | solution.py:316
  11.0 4.5 %packed.2.blocks = bf16[64,64,512]{2,1,0:T(8,128)(2,1)S(1)} custom-call(bf16[64,7,64,64]{3,2,1,0:T(8,128)(2,1)} %off.2, bf16[64,64,64]{2,1,0:T(8,128)(2,1)} %diag.2), custom_call_target="tpu_custom_call" | custom-call | bytes 12582912 | tf_op jit(solution)/shard_map/packed/pallas_call | solution.py:93
  15.5 4.6 %collective-permute-done.first_part = bf16[32,64,128]{2,1,0:T(8,128)(2,1)S(1)} collective-permute-done((bf16[32,64,128]{2,1,0:T(8,128)(2,1)S(1)}, bf16[32,64,128]{2,1,0:T(8,128)(2,1)S(1)}, u32[]{:S(2)}, u32[]{:S(2)}) %collective-permute-start) | collective-permute-done | bytes 524320 | tf_op jit(solution)/shard_map/ppermute | solution.py:315
  20.1 2.0 %second_lower.1 = (f32[32,64,128]{2,1,0:T(8,128)S(1)}, bf16[32,64,128]{2,1,0:T(8,128)(2,1)S(1)}) custom-call(s32[7,64]{1,0:T(8,128)S(1)} %bitcast.2, bf16[32,64,128]{2,1,0:T(8,128)(2,1)S(1)} %collective-permute-done.first_part, bf16[32,64,128]{2,1,0:T(8,128)(2,1)S(1)} %get-tuple-element.16.middle.first_part, ...), custom_call_target="tpu_custom_call" | custom-call | flops 335544320 | bytes 6029312 | tf_op jit(solution)/shard_map/second_lower/pallas_call | solution.py:155
  22.2 1.9 %collective-permute-start.3 = (bf16[32,64,128]{2,1,0:T(8,128)(2,1)S(1)}, bf16[32,64,128]{2,1,0:T(8,128)(2,1)S(1)}, u32[]{:S(2)}, u32[]{:S(2)}) collective-permute-start(bf16[32,64,128]{2,1,0:T(8,128)(2,1)S(1)} %get-tuple-element.20.first_part.middle), channel_id=1, source_target_pairs={{1,0},{2,1},{3,2},{4,3},{5,4},{6,5},{7,6},{8,7},{9,8},{10,9},{11,1... | collective-permute-start | bytes 1572872 | tf_op jit(solution)/shard_map/ppermute | solution.py:316
  24.1 2.0 %second_upper.1 = (f32[32,64,128]{2,1,0:T(8,128)S(1)}, bf16[32,64,128]{2,1,0:T(8,128)(2,1)S(1)}) custom-call(s32[7,64]{1,0:T(8,128)S(1)} %bitcast.3, bf16[32,64,128]{2,1,0:T(8,128)(2,1)S(1)} %get-tuple-element.16.middle.first_part, bf16[32,64,128]{2,1,0:T(8,128)(2,1)S(1)} %get-tuple-element.15.last_part.middle, ...), custom_call_target="tpu_custom_call" | custom-call | flops 335544320 | bytes 6029312 | tf_op jit(solution)/shard_map/second_upper/pallas_call | solution.py:155
  26.2 3.4 %collective-permute-start.2 = (bf16[32,64,128]{2,1,0:T(8,128)(2,1)S(1)}, bf16[32,64,128]{2,1,0:T(8,128)(2,1)S(1)}, u32[]{:S(2)}, u32[]{:S(2)}) collective-permute-start(bf16[32,64,128]{2,1,0:T(8,128)(2,1)S(1)} %get-tuple-element.19.middle.last_part), channel_id=1, source_target_pairs={{0,1},{1,2},{2,3},{3,4},{4,5},{5,6},{6,7},{7,8},{8,9},{9,10},{10,1... | collective-permute-start | bytes 1572872 | tf_op jit(solution)/shard_map/ppermute | solution.py:315
  29.5 6.4 %collective-permute-done.3.last_part = bf16[32,64,128]{2,1,0:T(8,128)(2,1)S(1)} collective-permute-done((bf16[32,64,128]{2,1,0:T(8,128)(2,1)S(1)}, bf16[32,64,128]{2,1,0:T(8,128)(2,1)S(1)}, u32[]{:S(2)}, u32[]{:S(2)}) %collective-permute-start.3) | collective-permute-done | bytes 524320 | tf_op jit(solution)/shard_map/ppermute | solution.py:316
  36.0 1.9 %restrict_upper.1.rest_0_ = f32[64,64,128]{2,1,0:T(8,128)S(1)} custom-call(s32[7,64]{1,0:T(8,128)S(1)} %bitcast.4, s32[64]{0:T(128)S(1)} %copy-done.4, bf16[32,64,128]{2,1,0:T(8,128)(2,1)S(1)} %get-tuple-element.20.first_part.middle, bf16[32,64,128]{2,1,0:T(8,128)(2,1)S(1)} %get-tuple-element.19.middle.last_part, ...), custom_call_target="tpu_custom_call" | custom-call | flops 268435456 | bytes 5242880 | tf_op jit(solution)/shard_map/restrict_upper/pallas_call | solution.py:189
  37.9 5.4 %collective-permute-done.2.first_part = bf16[32,64,128]{2,1,0:T(8,128)(2,1)S(1)} collective-permute-done((bf16[32,64,128]{2,1,0:T(8,128)(2,1)S(1)}, bf16[32,64,128]{2,1,0:T(8,128)(2,1)S(1)}, u32[]{:S(2)}, u32[]{:S(2)}) %collective-permute-start.2) | collective-permute-done | bytes 524320 | tf_op jit(solution)/shard_map/ppermute | solution.py:315
  43.3 1.7 %restrict_lower.1 = f32[64,64,128]{2,1,0:T(8,128)S(1)} custom-call(s32[7,64]{1,0:T(8,128)S(1)} %bitcast.5, s32[64]{0:T(128)S(1)} %copy-done.4, bf16[32,64,128]{2,1,0:T(8,128)(2,1)S(1)} %collective-permute-done.2.first_part, bf16[32,64,128]{2,1,0:T(8,128)(2,1)S(1)} %get-tuple-element.20.first_part.middle, ...), custom_call_target="tpu_custom_call", output_to_operand_aliasing={{}: (7, {})} | custom-call | flops 268435456 | bytes 5242880 | tf_op jit(solution)/shard_map/restrict_lower/pallas_call | solution.py:189
  45.1 2.6 %collective-permute-start.4 = (f32[32,64,128]{2,1,0:T(8,128)S(1)}, f32[32,64,128]{2,1,0:T(8,128)S(1)}, u32[]{:S(2)}, u32[]{:S(2)}) collective-permute-start(f32[32,64,128]{2,1,0:T(8,128)S(1)} %slice.17), channel_id=1, source_target_pairs={{0,32},{32,0},{64,96},{96,64},{128,160},{160,128},{192,224},{224,1... | collective-permute-start | bytes 3145736 | tf_op jit(solution)/shard_map/ppermute | solution.py:332
  47.7 2.3 %collective-permute-done.4 = f32[32,64,128]{2,1,0:T(8,128)S(1)} collective-permute-done((f32[32,64,128]{2,1,0:T(8,128)S(1)}, f32[32,64,128]{2,1,0:T(8,128)S(1)}, u32[]{:S(2)}, u32[]{:S(2)}) %collective-permute-start.4) | collective-permute-done | bytes 1048608 | tf_op jit(solution)/shard_map/ppermute | solution.py:332
  50.0 0.2 slice_add_fusion
  50.2 2.8 %collective-permute-start.6 = (bf16[16,64,128]{2,1,0:T(8,128)(2,1)S(1)}, bf16[16,64,128]{2,1,0:T(8,128)(2,1)S(1)}, u32[]{:S(2)}, u32[]{:S(2)}) collective-permute-start(bf16[16,64,128]{2,1,0:T(8,128)(2,1)S(1)} %get-tuple-element.31), channel_id=1, source_target_pairs={{0,192},{32,224},{64,128},{96,160},{128,64},{160,96},{192,0},{224,... | collective-permute-start | bytes 786440 | tf_op jit(solution)/shard_map/ppermute | solution.py:336
  53.0 6.1 %collective-permute-done.6 = bf16[16,64,128]{2,1,0:T(8,128)(2,1)S(1)} collective-permute-done((bf16[16,64,128]{2,1,0:T(8,128)(2,1)S(1)}, bf16[16,64,128]{2,1,0:T(8,128)(2,1)S(1)}, u32[]{:S(2)}, u32[]{:S(2)}) %collective-permute-start.6) | collective-permute-done | bytes 262176 | tf_op jit(solution)/shard_map/ppermute | solution.py:336
  59.2 1.1 %collective-permute-done.5 = bf16[16,64,128]{2,1,0:T(8,128)(2,1)S(1)} collective-permute-done((bf16[16,64,128]{2,1,0:T(8,128)(2,1)S(1)}, bf16[16,64,128]{2,1,0:T(8,128)(2,1)S(1)}, u32[]{:S(2)}, u32[]{:S(2)}) %collective-permute-start.5) | collective-permute-done | bytes 262176 | tf_op jit(solution)/shard_map/ppermute | solution.py:335
  60.2 0.2 fusion
  60.5 0.3 collective-permute-start.8
  60.7 1.5 %collective-permute-start.7 = (bf16[16,64,128]{2,1,0:T(8,128)(2,1)S(1)}, bf16[16,64,128]{2,1,0:T(8,128)(2,1)S(1)}, u32[]{:S(2)}, u32[]{:S(2)}) collective-permute-start(bf16[16,64,128]{2,1,0:T(8,128)(2,1)S(1)} %get-tuple-element.29), channel_id=1, source_target_pairs={{0,192},{32,224},{64,128},{96,160},{128,64},{160,96},{192,0},{224,... | collective-permute-start | bytes 786440 | tf_op jit(solution)/shard_map/ppermute | solution.py:338
  62.2 4.5 %packed.3.blocks = bf16[64,64,512]{2,1,0:T(8,128)(2,1)S(1)} custom-call(bf16[64,7,64,64]{3,2,1,0:T(8,128)(2,1)} %off.3, bf16[64,64,64]{2,1,0:T(8,128)(2,1)} %diag.3), custom_call_target="tpu_custom_call" | custom-call | bytes 12582912 | tf_op jit(solution)/shard_map/packed/pallas_call | solution.py:93
  66.8 1.3 %collective-permute-done.7.more_upper = bf16[16,64,128]{2,1,0:T(8,128)(2,1)S(1)} collective-permute-done((bf16[16,64,128]{2,1,0:T(8,128)(2,1)S(1)}, bf16[16,64,128]{2,1,0:T(8,128)(2,1)S(1)}, u32[]{:S(2)}, u32[]{:S(2)}) %collective-permute-start.7) | collective-permute-done | bytes 262176 | tf_op jit(solution)/shard_map/ppermute | solution.py:338
  68.1 0.3 coarse_first.1
  68.4 1.9 %collective-permute-start.9 = (bf16[32,64,128]{2,1,0:T(8,128)(2,1)S(1)}, bf16[32,64,128]{2,1,0:T(8,128)(2,1)S(1)}, u32[]{:S(2)}, u32[]{:S(2)}) collective-permute-start(bf16[32,64,128]{2,1,0:T(8,128)(2,1)S(1)} %get-tuple-element.22.own), channel_id=1, source_target_pairs={{2,1},{1,2},{4,3},{3,4},{6,5},{5,6},{8,7},{7,8},{10,9},{9,10},{12,... | collective-permute-start | bytes 1572872 | tf_op jit(solution)/shard_map/ppermute | solution.py:348
  70.3 2.6 %collective-permute-start.10 = (bf16[32,64,128]{2,1,0:T(8,128)(2,1)S(1)}, bf16[32,64,128]{2,1,0:T(8,128)(2,1)S(1)}, u32[]{:S(2)}, u32[]{:S(2)}) collective-permute-start(bf16[32,64,128]{2,1,0:T(8,128)(2,1)S(1)} %get-tuple-element.22.own), channel_id=1, source_target_pairs={{0,32},{32,0},{64,96},{96,64},{128,160},{160,128},{192,224},{224,1... | collective-permute-start | bytes 1572872 | tf_op jit(solution)/shard_map/ppermute | solution.py:350
  73.0 5.4 %collective-permute-done.9.halo = bf16[32,64,128]{2,1,0:T(8,128)(2,1)S(1)} collective-permute-done((bf16[32,64,128]{2,1,0:T(8,128)(2,1)S(1)}, bf16[32,64,128]{2,1,0:T(8,128)(2,1)S(1)}, u32[]{:S(2)}, u32[]{:S(2)}) %collective-permute-start.9) | collective-permute-done | bytes 524320 | tf_op jit(solution)/shard_map/ppermute | solution.py:348
  78.3 2.0 %coarse_second.1.kept = f32[32,64,128]{2,1,0:T(8,128)S(1)} custom-call(s32[7,64]{1,0:T(8,128)S(1)} %bitcast.6, bf16[32,64,128]{2,1,0:T(8,128)(2,1)S(1)} %collective-permute-done.9.halo, bf16[32,64,128]{2,1,0:T(8,128)(2,1)S(1)} %get-tuple-element.22.own, bf16[32,64,128]{2,1,0:T(8,128)(2,1)S(1)} %collective-permute-done.10.other, ...), custom_call_target="tpu_custom_call" | custom-call | flops 335544320 | bytes 6029312 | tf_op jit(solution)/shard_map/coarse_second/pallas_call | solution.py:251
  80.4 7.1 %collective-permute-start.11 = (f32[32,64,128]{2,1,0:T(8,128)S(1)}, f32[32,64,128]{2,1,0:T(8,128)S(1)}, u32[]{:S(2)}, u32[]{:S(2)}) collective-permute-start(f32[32,64,128]{2,1,0:T(8,128)S(1)} %coarse_second.1.kept), channel_id=1, source_target_pairs={{0,32},{32,0},{64,96},{96,64},{128,160},{160,128},{192,224},{224,1... | collective-permute-start | bytes 3145736 | tf_op jit(solution)/shard_map/ppermute | solution.py:360
  87.5 2.3 %collective-permute-done.11.given = f32[32,64,128]{2,1,0:T(8,128)S(1)} collective-permute-done((f32[32,64,128]{2,1,0:T(8,128)S(1)}, f32[32,64,128]{2,1,0:T(8,128)S(1)}, u32[]{:S(2)}, u32[]{:S(2)}) %collective-permute-start.11) | collective-permute-done | bytes 1048608 | tf_op jit(solution)/shard_map/ppermute | solution.py:360
  89.8 2.0 %corrected.1 = f32[64,64,128]{2,1,0:T(8,128)} custom-call(s32[64]{0:T(128)S(1)} %copy-done.4, f32[32,64,128]{2,1,0:T(8,128)S(1)} %get-tuple-element.17.lower, f32[32,64,128]{2,1,0:T(8,128)S(1)} %get-tuple-element.18.upper, f32[32,64,128]{2,1,0:T(8,128)S(1)} %coarse_second.1.kept, f32[32,64,128]{2,1,0:T(8,128)S(1)} %collective-permute-done.11.given), custom_call_target="tpu_custom_call" | custom-call | flops 524288 | bytes 6291456 | tf_op jit(solution)/shard_map/corrected/pallas_call | solution.py:283
  (18 shorter events, 0.3 us)
Async XLA Ops:
  2.1 18.0 %collective-permute-start = (bf16[32,64,128]{2,1,0:T(8,128)(2,1)S(1)}, bf16[32,64,128]{2,1,0:T(8,128)(2,1)S(1)}, u32[]{:S(2)}, u32[]{:S(2)}) collective-permute-start(bf16[32,64,128]{2,1,0:T(8,128)(2,1)S(1)} %get-tuple-element.15.last_part.middle), channel_id=1, source_target_pairs={{0,1},{1,2},{2,3},{3,4},{4,5},{5,6},{6,7},{7,8},{8,9},{9,10},{10,1... | collective-permute-start | bytes 1572872 | tf_op jit(solution)/shard_map/ppermute | solution.py:315
  5.3 14.9 %copy-start = (f32[64,64,128]{2,1,0:T(8,128)S(1)}, f32[64,64,128]{2,1,0:T(8,128)}, u32[]{:S(2)}) copy-start(f32[64,64,128]{2,1,0:T(8,128)} %rhs.9) | copy-start | bytes 6291460
  5.3 14.9 %copy-start.1 = (bf16[64,64,64]{2,1,0:T(8,128)(2,1)S(1)}, bf16[64,64,64]{2,1,0:T(8,128)(2,1)}, u32[]{:S(2)}) copy-start(bf16[64,64,64]{2,1,0:T(8,128)(2,1)} %smoother.7) | copy-start | bytes 1572868
  5.3 14.9 %copy-start.3 = (s32[64,7]{0,1:T(8,128)S(1)}, s32[64,7]{0,1:T(8,128)}, u32[]{:S(2)}) copy-start(s32[64,7]{0,1:T(8,128)} %param.14) | copy-start | bytes 5380
  5.3 18.8 %collective-permute-start.1 = (bf16[32,64,128]{2,1,0:T(8,128)(2,1)S(1)}, bf16[32,64,128]{2,1,0:T(8,128)(2,1)S(1)}, u32[]{:S(2)}, u32[]{:S(2)}) collective-permute-start(bf16[32,64,128]{2,1,0:T(8,128)(2,1)S(1)} %get-tuple-element.16.middle.first_part), channel_id=1, source_target_pairs={{1,0},{2,1},{3,2},{4,3},{5,4},{6,5},{7,6},{8,7},{9,8},{10,9},{11,1... | collective-permute-start | bytes 1572872 | tf_op jit(solution)/shard_map/ppermute | solution.py:316
  22.2 13.8 %copy-start.4 = (s32[64]{0:T(128)S(1)}, s32[64]{0:T(128)}, u32[]{:S(2)}) copy-start(s32[64]{0:T(128)} %aggregate.5) | copy-start | bytes 772
  22.2 13.8 %collective-permute-start.3 = (bf16[32,64,128]{2,1,0:T(8,128)(2,1)S(1)}, bf16[32,64,128]{2,1,0:T(8,128)(2,1)S(1)}, u32[]{:S(2)}, u32[]{:S(2)}) collective-permute-start(bf16[32,64,128]{2,1,0:T(8,128)(2,1)S(1)} %get-tuple-element.20.first_part.middle), channel_id=1, source_target_pairs={{1,0},{2,1},{3,2},{4,3},{5,4},{6,5},{7,6},{8,7},{9,8},{10,9},{11,1... | collective-permute-start | bytes 1572872 | tf_op jit(solution)/shard_map/ppermute | solution.py:316
  26.2 17.1 %collective-permute-start.2 = (bf16[32,64,128]{2,1,0:T(8,128)(2,1)S(1)}, bf16[32,64,128]{2,1,0:T(8,128)(2,1)S(1)}, u32[]{:S(2)}, u32[]{:S(2)}) collective-permute-start(bf16[32,64,128]{2,1,0:T(8,128)(2,1)S(1)} %get-tuple-element.19.middle.last_part), channel_id=1, source_target_pairs={{0,1},{1,2},{2,3},{3,4},{4,5},{5,6},{6,7},{7,8},{8,9},{9,10},{10,1... | collective-permute-start | bytes 1572872 | tf_op jit(solution)/shard_map/ppermute | solution.py:315
  45.1 4.8 %collective-permute-start.4 = (f32[32,64,128]{2,1,0:T(8,128)S(1)}, f32[32,64,128]{2,1,0:T(8,128)S(1)}, u32[]{:S(2)}, u32[]{:S(2)}) collective-permute-start(f32[32,64,128]{2,1,0:T(8,128)S(1)} %slice.17), channel_id=1, source_target_pairs={{0,32},{32,0},{64,96},{96,64},{128,160},{160,128},{192,224},{224,1... | collective-permute-start | bytes 3145736 | tf_op jit(solution)/shard_map/ppermute | solution.py:332
  50.2 9.0 %collective-permute-start.6 = (bf16[16,64,128]{2,1,0:T(8,128)(2,1)S(1)}, bf16[16,64,128]{2,1,0:T(8,128)(2,1)S(1)}, u32[]{:S(2)}, u32[]{:S(2)}) collective-permute-start(bf16[16,64,128]{2,1,0:T(8,128)(2,1)S(1)} %get-tuple-element.31), channel_id=1, source_target_pairs={{0,192},{32,224},{64,128},{96,160},{128,64},{160,96},{192,0},{224,... | collective-permute-start | bytes 786440 | tf_op jit(solution)/shard_map/ppermute | solution.py:336
  53.0 7.2 %collective-permute-start.5 = (bf16[16,64,128]{2,1,0:T(8,128)(2,1)S(1)}, bf16[16,64,128]{2,1,0:T(8,128)(2,1)S(1)}, u32[]{:S(2)}, u32[]{:S(2)}) collective-permute-start(bf16[16,64,128]{2,1,0:T(8,128)(2,1)S(1)} %get-tuple-element.32), channel_id=1, source_target_pairs={{0,64},{32,96},{64,0},{96,32},{128,192},{160,224},{192,128},{224,1... | collective-permute-start | bytes 786440 | tf_op jit(solution)/shard_map/ppermute | solution.py:335
  60.5 6.4 %collective-permute-start.8 = (bf16[16,64,128]{2,1,0:T(8,128)(2,1)S(1)}, bf16[16,64,128]{2,1,0:T(8,128)(2,1)S(1)}, u32[]{:S(2)}, u32[]{:S(2)}) collective-permute-start(bf16[16,64,128]{2,1,0:T(8,128)(2,1)S(1)} %get-tuple-element.25), channel_id=1, source_target_pairs={{0,64},{32,96},{64,0},{96,32},{128,192},{160,224},{192,128},{224,1... | collective-permute-start | bytes 786440 | tf_op jit(solution)/shard_map/ppermute | solution.py:339
  60.7 7.4 %copy-start.2 = (bf16[64,64,64]{2,1,0:T(8,128)(2,1)S(1)}, bf16[64,64,64]{2,1,0:T(8,128)(2,1)}, u32[]{:S(2)}) copy-start(bf16[64,64,64]{2,1,0:T(8,128)(2,1)} %smoother.9) | copy-start | bytes 1572868
  60.7 7.4 %collective-permute-start.7 = (bf16[16,64,128]{2,1,0:T(8,128)(2,1)S(1)}, bf16[16,64,128]{2,1,0:T(8,128)(2,1)S(1)}, u32[]{:S(2)}, u32[]{:S(2)}) collective-permute-start(bf16[16,64,128]{2,1,0:T(8,128)(2,1)S(1)} %get-tuple-element.29), channel_id=1, source_target_pairs={{0,192},{32,224},{64,128},{96,160},{128,64},{160,96},{192,0},{224,... | collective-permute-start | bytes 786440 | tf_op jit(solution)/shard_map/ppermute | solution.py:338
  66.7 11.6 %copy-start.5 = (s32[64,7]{0,1:T(8,128)S(1)}, s32[64,7]{0,1:T(8,128)}, u32[]{:S(2)}) copy-start(s32[64,7]{0,1:T(8,128)} %param.19) | copy-start | bytes 5380
  68.4 9.9 %collective-permute-start.9 = (bf16[32,64,128]{2,1,0:T(8,128)(2,1)S(1)}, bf16[32,64,128]{2,1,0:T(8,128)(2,1)S(1)}, u32[]{:S(2)}, u32[]{:S(2)}) collective-permute-start(bf16[32,64,128]{2,1,0:T(8,128)(2,1)S(1)} %get-tuple-element.22.own), channel_id=1, source_target_pairs={{2,1},{1,2},{4,3},{3,4},{6,5},{5,6},{8,7},{7,8},{10,9},{9,10},{12,... | collective-permute-start | bytes 1572872 | tf_op jit(solution)/shard_map/ppermute | solution.py:348
  70.3 8.0 %collective-permute-start.10 = (bf16[32,64,128]{2,1,0:T(8,128)(2,1)S(1)}, bf16[32,64,128]{2,1,0:T(8,128)(2,1)S(1)}, u32[]{:S(2)}, u32[]{:S(2)}) collective-permute-start(bf16[32,64,128]{2,1,0:T(8,128)(2,1)S(1)} %get-tuple-element.22.own), channel_id=1, source_target_pairs={{0,32},{32,0},{64,96},{96,64},{128,160},{160,128},{192,224},{224,1... | collective-permute-start | bytes 1572872 | tf_op jit(solution)/shard_map/ppermute | solution.py:350
  80.4 9.4 %collective-permute-start.11 = (f32[32,64,128]{2,1,0:T(8,128)S(1)}, f32[32,64,128]{2,1,0:T(8,128)S(1)}, u32[]{:S(2)}, u32[]{:S(2)}) collective-permute-start(f32[32,64,128]{2,1,0:T(8,128)S(1)} %coarse_second.1.kept), channel_id=1, source_target_pairs={{0,32},{32,0},{64,96},{96,64},{128,160},{160,128},{192,224},{224,1... | collective-permute-start | bytes 3145736 | tf_op jit(solution)/shard_map/ppermute | solution.py:360

commit v3 on v2

--- a/solution.py
+++ b/solution.py
@@ -41,15 +41,15 @@
     return pltpu.with_memory_space_constraint(array, pltpu.HBM)
 
 
-def first_kernel(step, smoother, rhs, low, high, smoother_here, rhs_here, sem):
-    n, half = rhs.shape[0], low.shape[0]
+def first_kernel(step, start, smoother, rhs, out, smoother_here, rhs_here, sem):
+    n = out.shape[0]
     copies = []
     for s in range(0, n, step):
-        rows = slice(s, s + step)
+        here, there = slice(s, s + step), slice(start + s, start + s + step)
         k = 2 * (s // step)
         pair = (
-            pltpu.make_async_copy(smoother.at[rows], smoother_here.at[rows], sem.at[k]),
-            pltpu.make_async_copy(rhs.at[rows], rhs_here.at[rows], sem.at[k + 1]),
+            pltpu.make_async_copy(smoother.at[there], smoother_here.at[here], sem.at[k]),
+            pltpu.make_async_copy(rhs.at[there], rhs_here.at[here], sem.at[k + 1]),
         )
         for c in pair:
             c.start()
@@ -59,26 +59,25 @@
             c.wait()
         products = [dot(smoother_here[r], rhs_here[r].astype(bf16)) for r in range(s, s + step)]
         for r in range(s, s + step):
-            out = low if r < half else high
-            out[r % half] = (damping * products[r - s]).astype(bf16)
-
-
-def first_iterate(smoother, rhs):
+            out[r] = (damping * products[r - s]).astype(bf16)
+
+
+def first_iterate(upper, smoother, rhs):
     n, b, k = rhs.shape
-    step = 16
-    return pl.pallas_call(
-        functools.partial(first_kernel, step),
+    half, step = n // 2, 16
+    return pl.pallas_call(
+        functools.partial(first_kernel, step, half if upper else 0),
         in_specs=[hbm, hbm],
-        out_specs=[vmem, vmem],
-        out_shape=[shape(bf16, n // 2, b, k)] * 2,
+        out_specs=vmem,
+        out_shape=shape(bf16, half, b, k),
         scratch_shapes=[
-            pltpu.VMEM((n, b, b), bf16),
-            pltpu.VMEM((n, b, k), f32),
-            pltpu.SemaphoreType.DMA((2 * n // step,)),
+            pltpu.VMEM((half, b, b), bf16),
+            pltpu.VMEM((half, b, k), f32),
+            pltpu.SemaphoreType.DMA((2 * half // step,)),
         ],
         compiler_params=params(16),
-        cost_estimate=cost(2 * n * b * b * k, 6 * n * b * k + 4 * n * b * b),
-        name="first_iterate",
+        cost_estimate=cost(n * b * b * k, 3 * n * b * k + 2 * n * b * b),
+        name="first_upper" if upper else "first_lower",
     )(in_hbm(smoother), in_hbm(rhs))
 
 
@@ -315,8 +314,10 @@
     to_next = lambda v: lax.ppermute(v, fine_axes, [(i, i + 1) for i in ends])
     to_previous = lambda v: lax.ppermute(v, fine_axes, [(i + 1, i) for i in ends])
 
-    low, high = first_iterate(fine_smoother, rhs)
-    before, after = to_next(high), to_previous(low)
+    high = first_iterate(True, fine_smoother, rhs)
+    before = to_next(high)
+    low = first_iterate(False, fine_smoother, rhs)
+    after = to_previous(low)
     fine = packed(fine_blocks, fine_diag)
     lower, low2 = second_iterate(False, fine_cols, (before, low, high), fine, fine_smoother, rhs)
     after2 = to_previous(low2)

time: 92 us -> 91.5 us (level)
  waiting for transfers between devices: 34.9 us -> 32 us
  starting transfers between devices: 33 us -> 34.2 us
  Pallas kernels: 23.1 us -> 24.2 us
    ppermute x2, waiting for transfers between devices: 9.99 us -> 8.36 us  [on_device(): to_next = lambda v: lax.ppermute(v, fine_axes, [(i, i + 1) for i in ends])]
    ppermute x1, waiting for transfers between devices: 5.35 us -> 4.11 us  [on_device(): halo = lax.ppermute(rounded_first, fine_axes, towards)]
    ppermute x1, starting transfers between devices: 2.65 us -> 3.89 us  [on_device(): other = lax.ppermute(own, 'grp', across)]
    pallas_call x1 -> x2, Pallas kernels: 2.12 us -> 3.22 us  [first_iterate(): pl.pallas_call(functools.partial(first_kernel, step, half if upper else 0...]
  transfers between devices with their start and end apart: 12 -> 12, of which waited for: 10 -> 10; matrix products, arithmetic and copies ran while one was open for 0% -> 0% of each run, Pallas kernels for 16% -> 18%
where the time goes in v3:
time: 91.5 us; the launch traced here: 91.2 us
  starting transfers between devices  34.2 us (37%)
  waiting for transfers between devices  32 us (35%)
  Pallas kernels  24.2 us (26%)
    pallas_call x2, Pallas kernels, packed(): pl.pallas_call(functools.partial(pack_kernel, step), grid=(rows // step,)...  8.97 us
    ppermute x2, waiting for transfers between devices, on_device(): to_next = lambda v: lax.ppermute(v, fine_axes, [(i, i + 1) for i in ends])  8.36 us
    ppermute x2, starting transfers between devices, on_device(): lax.ppermute(v, fine_axes, [(i + 1, i) for i in ends])  7.67 us
    ppermute x1, starting transfers between devices, on_device(): theirs = lax.ppermute(mine, 'grp', across)  7.12 us
    ppermute x2, starting transfers between devices, on_device(): to_next = lambda v: lax.ppermute(v, fine_axes, [(i, i + 1) for i in ends])  6.48 us
    ppermute x2, waiting for transfers between devices, on_device(): lax.ppermute(v, fine_axes, [(i + 1, i) for i in ends])  6.41 us
    ppermute x1, waiting for transfers between devices, on_device(): from_two = lax.ppermute(two.astype(bf16), 'grp', far)  6.13 us
    ppermute x1, waiting for transfers between devices, on_device(): halo = lax.ppermute(rounded_first, fine_axes, towards)  4.11 us
  transfers between devices with their start and end apart: 12, of which 10 were waited for; matrix products, arithmetic and copies ran while one was open for 0% of the time, Pallas kernels for 18%

profile of v3, /device:TPU:129, one launch (start us, length us, event | category | flops | bytes accessed | tf_op | source)
XLA Modules:
  0.0 91.2 jit_solution(4505848285343404706)
XLA Ops:
  0.0 1.6 %first_upper.1.last_part.middle = bf16[32,64,128]{2,1,0:T(8,128)(2,1)S(1)} custom-call(bf16[64,64,64]{2,1,0:T(8,128)(2,1)} %smoother.9, f32[64,64,128]{2,1,0:T(8,128)} %rhs.11), custom_call_target="tpu_custom_call" | custom-call | flops 33554432 | bytes 2097152 | tf_op jit(solution)/shard_map/first_upper/pallas_call | solution.py:68
  1.6 3.1 %collective-permute-start = (bf16[32,64,128]{2,1,0:T(8,128)(2,1)S(1)}, bf16[32,64,128]{2,1,0:T(8,128)(2,1)S(1)}, u32[]{:S(2)}, u32[]{:S(2)}) collective-permute-start(bf16[32,64,128]{2,1,0:T(8,128)(2,1)S(1)} %first_upper.1.last_part.middle), channel_id=1, source_target_pairs={{0,1},{1,2},{2,3},{3,4},{4,5},{5,6},{6,7},{7,8},{8,9},{9,10},{10,1... | collective-permute-start | bytes 1572872 | tf_op jit(solution)/shard_map/ppermute | solution.py:314
  4.7 1.6 %first_lower.1.middle.first_part = bf16[32,64,128]{2,1,0:T(8,128)(2,1)S(1)} custom-call(bf16[64,64,64]{2,1,0:T(8,128)(2,1)} %smoother.9, f32[64,64,128]{2,1,0:T(8,128)} %rhs.11), custom_call_target="tpu_custom_call" | custom-call | flops 33554432 | bytes 2097152 | tf_op jit(solution)/shard_map/first_lower/pallas_call | solution.py:68
  6.4 5.7 %collective-permute-start.1 = (bf16[32,64,128]{2,1,0:T(8,128)(2,1)S(1)}, bf16[32,64,128]{2,1,0:T(8,128)(2,1)S(1)}, u32[]{:S(2)}, u32[]{:S(2)}) collective-permute-start(bf16[32,64,128]{2,1,0:T(8,128)(2,1)S(1)} %first_lower.1.middle.first_part), channel_id=1, source_target_pairs={{1,0},{2,1},{3,2},{4,3},{5,4},{6,5},{7,6},{8,7},{9,8},{10,9},{11,1... | collective-permute-start | bytes 1572872 | tf_op jit(solution)/shard_map/ppermute | solution.py:315
  12.2 4.5 %packed.2.blocks = bf16[64,64,512]{2,1,0:T(8,128)(2,1)S(1)} custom-call(bf16[64,7,64,64]{3,2,1,0:T(8,128)(2,1)} %off.2, bf16[64,64,64]{2,1,0:T(8,128)(2,1)} %diag.2), custom_call_target="tpu_custom_call" | custom-call | bytes 12582912 | tf_op jit(solution)/shard_map/packed/pallas_call | solution.py:92
  16.7 3.0 %collective-permute-done.first_part = bf16[32,64,128]{2,1,0:T(8,128)(2,1)S(1)} collective-permute-done((bf16[32,64,128]{2,1,0:T(8,128)(2,1)S(1)}, bf16[32,64,128]{2,1,0:T(8,128)(2,1)S(1)}, u32[]{:S(2)}, u32[]{:S(2)}) %collective-permute-start) | collective-permute-done | bytes 524320 | tf_op jit(solution)/shard_map/ppermute | solution.py:314
  19.6 2.0 %second_lower.1 = (f32[32,64,128]{2,1,0:T(8,128)S(1)}, bf16[32,64,128]{2,1,0:T(8,128)(2,1)S(1)}) custom-call(s32[7,64]{1,0:T(8,128)S(1)} %bitcast.2, bf16[32,64,128]{2,1,0:T(8,128)(2,1)S(1)} %collective-permute-done.first_part, bf16[32,64,128]{2,1,0:T(8,128)(2,1)S(1)} %first_lower.1.middle.first_part, bf16[32,64,128]{2,1,0:T(8,128)(2,1)S(1)} %first_upper.1.last_part.middle, ...), custom_call_target="tpu_custom_call" | custom-call | flops 335544320 | bytes 6029312 | tf_op jit(solution)/shard_map/second_lower/pallas_call | solution.py:154
  21.7 1.9 %collective-permute-start.3 = (bf16[32,64,128]{2,1,0:T(8,128)(2,1)S(1)}, bf16[32,64,128]{2,1,0:T(8,128)(2,1)S(1)}, u32[]{:S(2)}, u32[]{:S(2)}) collective-permute-start(bf16[32,64,128]{2,1,0:T(8,128)(2,1)S(1)} %get-tuple-element.16.first_part.middle), channel_id=1, source_target_pairs={{1,0},{2,1},{3,2},{4,3},{5,4},{6,5},{7,6},{8,7},{9,8},{10,9},{11,1... | collective-permute-start | bytes 1572872 | tf_op jit(solution)/shard_map/ppermute | solution.py:315
  23.6 2.0 %second_upper.1 = (f32[32,64,128]{2,1,0:T(8,128)S(1)}, bf16[32,64,128]{2,1,0:T(8,128)(2,1)S(1)}) custom-call(s32[7,64]{1,0:T(8,128)S(1)} %bitcast.3, bf16[32,64,128]{2,1,0:T(8,128)(2,1)S(1)} %first_lower.1.middle.first_part, bf16[32,64,128]{2,1,0:T(8,128)(2,1)S(1)} %first_upper.1.last_part.middle, bf16[32,64,128]{2,1,0:T(8,128)(2,1)S(1)} %collective-permute-done.1.last_part, ...), custom_call_target="tpu_custom_call" | custom-call | flops 335544320 | bytes 6029312 | tf_op jit(solution)/shard_map/second_upper/pallas_call | solution.py:154
  25.7 3.4 %collective-permute-start.2 = (bf16[32,64,128]{2,1,0:T(8,128)(2,1)S(1)}, bf16[32,64,128]{2,1,0:T(8,128)(2,1)S(1)}, u32[]{:S(2)}, u32[]{:S(2)}) collective-permute-start(bf16[32,64,128]{2,1,0:T(8,128)(2,1)S(1)} %get-tuple-element.15.middle.last_part), channel_id=1, source_target_pairs={{0,1},{1,2},{2,3},{3,4},{4,5},{5,6},{6,7},{7,8},{8,9},{9,10},{10,1... | collective-permute-start | bytes 1572872 | tf_op jit(solution)/shard_map/ppermute | solution.py:314
  29.0 6.4 %collective-permute-done.3.last_part = bf16[32,64,128]{2,1,0:T(8,128)(2,1)S(1)} collective-permute-done((bf16[32,64,128]{2,1,0:T(8,128)(2,1)S(1)}, bf16[32,64,128]{2,1,0:T(8,128)(2,1)S(1)}, u32[]{:S(2)}, u32[]{:S(2)}) %collective-permute-start.3) | collective-permute-done | bytes 524320 | tf_op jit(solution)/shard_map/ppermute | solution.py:315
  35.5 1.9 %restrict_upper.1.rest_0_ = f32[64,64,128]{2,1,0:T(8,128)S(1)} custom-call(s32[7,64]{1,0:T(8,128)S(1)} %bitcast.4, s32[64]{0:T(128)S(1)} %copy-done.4, bf16[32,64,128]{2,1,0:T(8,128)(2,1)S(1)} %get-tuple-element.16.first_part.middle, bf16[32,64,128]{2,1,0:T(8,128)(2,1)S(1)} %get-tuple-element.15.middle.last_part, ...), custom_call_target="tpu_custom_call" | custom-call | flops 268435456 | bytes 5242880 | tf_op jit(solution)/shard_map/restrict_upper/pallas_call | solution.py:188
  37.4 5.4 %collective-permute-done.2.first_part = bf16[32,64,128]{2,1,0:T(8,128)(2,1)S(1)} collective-permute-done((bf16[32,64,128]{2,1,0:T(8,128)(2,1)S(1)}, bf16[32,64,128]{2,1,0:T(8,128)(2,1)S(1)}, u32[]{:S(2)}, u32[]{:S(2)}) %collective-permute-start.2) | collective-permute-done | bytes 524320 | tf_op jit(solution)/shard_map/ppermute | solution.py:314
  42.8 1.7 %restrict_lower.1 = f32[64,64,128]{2,1,0:T(8,128)S(1)} custom-call(s32[7,64]{1,0:T(8,128)S(1)} %bitcast.5, s32[64]{0:T(128)S(1)} %copy-done.4, bf16[32,64,128]{2,1,0:T(8,128)(2,1)S(1)} %collective-permute-done.2.first_part, bf16[32,64,128]{2,1,0:T(8,128)(2,1)S(1)} %get-tuple-element.16.first_part.middle, ...), custom_call_target="tpu_custom_call", output_to_operand_aliasing={{}: (7, {})} | custom-call | flops 268435456 | bytes 5242880 | tf_op jit(solution)/shard_map/restrict_lower/pallas_call | solution.py:188
  44.6 2.6 %collective-permute-start.4 = (f32[32,64,128]{2,1,0:T(8,128)S(1)}, f32[32,64,128]{2,1,0:T(8,128)S(1)}, u32[]{:S(2)}, u32[]{:S(2)}) collective-permute-start(f32[32,64,128]{2,1,0:T(8,128)S(1)} %slice.17), channel_id=1, source_target_pairs={{0,32},{32,0},{64,96},{96,64},{128,160},{160,128},{192,224},{224,1... | collective-permute-start | bytes 3145736 | tf_op jit(solution)/shard_map/ppermute | solution.py:333
  47.2 2.3 %collective-permute-done.4 = f32[32,64,128]{2,1,0:T(8,128)S(1)} collective-permute-done((f32[32,64,128]{2,1,0:T(8,128)S(1)}, f32[32,64,128]{2,1,0:T(8,128)S(1)}, u32[]{:S(2)}, u32[]{:S(2)}) %collective-permute-start.4) | collective-permute-done | bytes 1048608 | tf_op jit(solution)/shard_map/ppermute | solution.py:333
  49.7 2.8 %collective-permute-start.6 = (bf16[16,64,128]{2,1,0:T(8,128)(2,1)S(1)}, bf16[16,64,128]{2,1,0:T(8,128)(2,1)S(1)}, u32[]{:S(2)}, u32[]{:S(2)}) collective-permute-start(bf16[16,64,128]{2,1,0:T(8,128)(2,1)S(1)} %get-tuple-element.27), channel_id=1, source_target_pairs={{0,192},{32,224},{64,128},{96,160},{128,64},{160,96},{192,0},{224,... | collective-permute-start | bytes 786440 | tf_op jit(solution)/shard_map/ppermute | solution.py:337
  52.5 6.1 %collective-permute-done.6 = bf16[16,64,128]{2,1,0:T(8,128)(2,1)S(1)} collective-permute-done((bf16[16,64,128]{2,1,0:T(8,128)(2,1)S(1)}, bf16[16,64,128]{2,1,0:T(8,128)(2,1)S(1)}, u32[]{:S(2)}, u32[]{:S(2)}) %collective-permute-start.6) | collective-permute-done | bytes 262176 | tf_op jit(solution)/shard_map/ppermute | solution.py:337
  58.7 1.1 %collective-permute-done.5 = bf16[16,64,128]{2,1,0:T(8,128)(2,1)S(1)} collective-permute-done((bf16[16,64,128]{2,1,0:T(8,128)(2,1)S(1)}, bf16[16,64,128]{2,1,0:T(8,128)(2,1)S(1)}, u32[]{:S(2)}, u32[]{:S(2)}) %collective-permute-start.5) | collective-permute-done | bytes 262176 | tf_op jit(solution)/shard_map/ppermute | solution.py:336
  59.7 0.2 fusion
  60.0 0.3 collective-permute-start.8
  60.2 1.5 %collective-permute-start.7 = (bf16[16,64,128]{2,1,0:T(8,128)(2,1)S(1)}, bf16[16,64,128]{2,1,0:T(8,128)(2,1)S(1)}, u32[]{:S(2)}, u32[]{:S(2)}) collective-permute-start(bf16[16,64,128]{2,1,0:T(8,128)(2,1)S(1)} %get-tuple-element.25), channel_id=1, source_target_pairs={{0,192},{32,224},{64,128},{96,160},{128,64},{160,96},{192,0},{224,... | collective-permute-start | bytes 786440 | tf_op jit(solution)/shard_map/ppermute | solution.py:339
  61.7 4.5 %packed.3.blocks = bf16[64,64,512]{2,1,0:T(8,128)(2,1)S(1)} custom-call(bf16[64,7,64,64]{3,2,1,0:T(8,128)(2,1)} %off.3, bf16[64,64,64]{2,1,0:T(8,128)(2,1)} %diag.3), custom_call_target="tpu_custom_call" | custom-call | bytes 12582912 | tf_op jit(solution)/shard_map/packed/pallas_call | solution.py:92
  66.3 1.3 %collective-permute-done.7.more_upper = bf16[16,64,128]{2,1,0:T(8,128)(2,1)S(1)} collective-permute-done((bf16[16,64,128]{2,1,0:T(8,128)(2,1)S(1)}, bf16[16,64,128]{2,1,0:T(8,128)(2,1)S(1)}, u32[]{:S(2)}, u32[]{:S(2)}) %collective-permute-start.7) | collective-permute-done | bytes 262176 | tf_op jit(solution)/shard_map/ppermute | solution.py:339
  67.6 0.3 coarse_first.1
  67.9 1.9 %collective-permute-start.9 = (bf16[32,64,128]{2,1,0:T(8,128)(2,1)S(1)}, bf16[32,64,128]{2,1,0:T(8,128)(2,1)S(1)}, u32[]{:S(2)}, u32[]{:S(2)}) collective-permute-start(bf16[32,64,128]{2,1,0:T(8,128)(2,1)S(1)} %get-tuple-element.18.own), channel_id=1, source_target_pairs={{2,1},{1,2},{4,3},{3,4},{6,5},{5,6},{8,7},{7,8},{10,9},{9,10},{12,... | collective-permute-start | bytes 1572872 | tf_op jit(solution)/shard_map/ppermute | solution.py:349
  69.8 3.9 %collective-permute-start.10 = (bf16[32,64,128]{2,1,0:T(8,128)(2,1)S(1)}, bf16[32,64,128]{2,1,0:T(8,128)(2,1)S(1)}, u32[]{:S(2)}, u32[]{:S(2)}) collective-permute-start(bf16[32,64,128]{2,1,0:T(8,128)(2,1)S(1)} %get-tuple-element.18.own), channel_id=1, source_target_pairs={{0,32},{32,0},{64,96},{96,64},{128,160},{160,128},{192,224},{224,1... | collective-permute-start | bytes 1572872 | tf_op jit(solution)/shard_map/ppermute | solution.py:351
  73.7 4.1 %collective-permute-done.9.halo = bf16[32,64,128]{2,1,0:T(8,128)(2,1)S(1)} collective-permute-done((bf16[32,64,128]{2,1,0:T(8,128)(2,1)S(1)}, bf16[32,64,128]{2,1,0:T(8,128)(2,1)S(1)}, u32[]{:S(2)}, u32[]{:S(2)}) %collective-permute-start.9) | collective-permute-done | bytes 524320 | tf_op jit(solution)/shard_map/ppermute | solution.py:349
  77.8 2.0 %coarse_second.1.kept = f32[32,64,128]{2,1,0:T(8,128)S(1)} custom-call(s32[7,64]{1,0:T(8,128)S(1)} %bitcast.6, bf16[32,64,128]{2,1,0:T(8,128)(2,1)S(1)} %collective-permute-done.9.halo, bf16[32,64,128]{2,1,0:T(8,128)(2,1)S(1)} %get-tuple-element.18.own, bf16[32,64,128]{2,1,0:T(8,128)(2,1)S(1)} %collective-permute-done.10.other, ...), custom_call_target="tpu_custom_call" | custom-call | flops 335544320 | bytes 6029312 | tf_op jit(solution)/shard_map/coarse_second/pallas_call | solution.py:250
  79.9 7.1 %collective-permute-start.11 = (f32[32,64,128]{2,1,0:T(8,128)S(1)}, f32[32,64,128]{2,1,0:T(8,128)S(1)}, u32[]{:S(2)}, u32[]{:S(2)}) collective-permute-start(f32[32,64,128]{2,1,0:T(8,128)S(1)} %coarse_second.1.kept), channel_id=1, source_target_pairs={{0,32},{32,0},{64,96},{96,64},{128,160},{160,128},{192,224},{224,1... | collective-permute-start | bytes 3145736 | tf_op jit(solution)/shard_map/ppermute | solution.py:361
  87.0 2.3 %collective-permute-done.11.given = f32[32,64,128]{2,1,0:T(8,128)S(1)} collective-permute-done((f32[32,64,128]{2,1,0:T(8,128)S(1)}, f32[32,64,128]{2,1,0:T(8,128)S(1)}, u32[]{:S(2)}, u32[]{:S(2)}) %collective-permute-start.11) | collective-permute-done | bytes 1048608 | tf_op jit(solution)/shard_map/ppermute | solution.py:361
  89.3 2.0 %corrected.1 = f32[64,64,128]{2,1,0:T(8,128)} custom-call(s32[64]{0:T(128)S(1)} %copy-done.4, f32[32,64,128]{2,1,0:T(8,128)S(1)} %get-tuple-element.13.lower, f32[32,64,128]{2,1,0:T(8,128)S(1)} %get-tuple-element.14.upper, f32[32,64,128]{2,1,0:T(8,128)S(1)} %coarse_second.1.kept, f32[32,64,128]{2,1,0:T(8,128)S(1)} %collective-permute-done.11.given), custom_call_target="tpu_custom_call" | custom-call | flops 524288 | bytes 6291456 | tf_op jit(solution)/shard_map/corrected/pallas_call | solution.py:282
  (19 shorter events, 0.5 us)
Async XLA Ops:
  1.6 18.0 %collective-permute-start = (bf16[32,64,128]{2,1,0:T(8,128)(2,1)S(1)}, bf16[32,64,128]{2,1,0:T(8,128)(2,1)S(1)}, u32[]{:S(2)}, u32[]{:S(2)}) collective-permute-start(bf16[32,64,128]{2,1,0:T(8,128)(2,1)S(1)} %first_upper.1.last_part.middle), channel_id=1, source_target_pairs={{0,1},{1,2},{2,3},{3,4},{4,5},{5,6},{6,7},{7,8},{8,9},{9,10},{10,1... | collective-permute-start | bytes 1572872 | tf_op jit(solution)/shard_map/ppermute | solution.py:314
  6.4 13.3 %copy-start = (f32[64,64,128]{2,1,0:T(8,128)S(1)}, f32[64,64,128]{2,1,0:T(8,128)}, u32[]{:S(2)}) copy-start(f32[64,64,128]{2,1,0:T(8,128)} %rhs.11) | copy-start | bytes 6291460
  6.4 13.2 %copy-start.1 = (bf16[64,64,64]{2,1,0:T(8,128)(2,1)S(1)}, bf16[64,64,64]{2,1,0:T(8,128)(2,1)}, u32[]{:S(2)}) copy-start(bf16[64,64,64]{2,1,0:T(8,128)(2,1)} %smoother.9) | copy-start | bytes 1572868
  6.4 13.2 %copy-start.3 = (s32[64,7]{0,1:T(8,128)S(1)}, s32[64,7]{0,1:T(8,128)}, u32[]{:S(2)}) copy-start(s32[64,7]{0,1:T(8,128)} %param.14) | copy-start | bytes 5380
  6.4 17.2 %collective-permute-start.1 = (bf16[32,64,128]{2,1,0:T(8,128)(2,1)S(1)}, bf16[32,64,128]{2,1,0:T(8,128)(2,1)S(1)}, u32[]{:S(2)}, u32[]{:S(2)}) collective-permute-start(bf16[32,64,128]{2,1,0:T(8,128)(2,1)S(1)} %first_lower.1.middle.first_part), channel_id=1, source_target_pairs={{1,0},{2,1},{3,2},{4,3},{5,4},{6,5},{7,6},{8,7},{9,8},{10,9},{11,1... | collective-permute-start | bytes 1572872 | tf_op jit(solution)/shard_map/ppermute | solution.py:315
  21.7 13.8 %copy-start.4 = (s32[64]{0:T(128)S(1)}, s32[64]{0:T(128)}, u32[]{:S(2)}) copy-start(s32[64]{0:T(128)} %aggregate.5) | copy-start | bytes 772
  21.7 13.8 %collective-permute-start.3 = (bf16[32,64,128]{2,1,0:T(8,128)(2,1)S(1)}, bf16[32,64,128]{2,1,0:T(8,128)(2,1)S(1)}, u32[]{:S(2)}, u32[]{:S(2)}) collective-permute-start(bf16[32,64,128]{2,1,0:T(8,128)(2,1)S(1)} %get-tuple-element.16.first_part.middle), channel_id=1, source_target_pairs={{1,0},{2,1},{3,2},{4,3},{5,4},{6,5},{7,6},{8,7},{9,8},{10,9},{11,1... | collective-permute-start | bytes 1572872 | tf_op jit(solution)/shard_map/ppermute | solution.py:315
  25.7 17.1 %collective-permute-start.2 = (bf16[32,64,128]{2,1,0:T(8,128)(2,1)S(1)}, bf16[32,64,128]{2,1,0:T(8,128)(2,1)S(1)}, u32[]{:S(2)}, u32[]{:S(2)}) collective-permute-start(bf16[32,64,128]{2,1,0:T(8,128)(2,1)S(1)} %get-tuple-element.15.middle.last_part), channel_id=1, source_target_pairs={{0,1},{1,2},{2,3},{3,4},{4,5},{5,6},{6,7},{7,8},{8,9},{9,10},{10,1... | collective-permute-start | bytes 1572872 | tf_op jit(solution)/shard_map/ppermute | solution.py:314
  44.6 4.8 %collective-permute-start.4 = (f32[32,64,128]{2,1,0:T(8,128)S(1)}, f32[32,64,128]{2,1,0:T(8,128)S(1)}, u32[]{:S(2)}, u32[]{:S(2)}) collective-permute-start(f32[32,64,128]{2,1,0:T(8,128)S(1)} %slice.17), channel_id=1, source_target_pairs={{0,32},{32,0},{64,96},{96,64},{128,160},{160,128},{192,224},{224,1... | collective-permute-start | bytes 3145736 | tf_op jit(solution)/shard_map/ppermute | solution.py:333
  49.7 9.0 %collective-permute-start.6 = (bf16[16,64,128]{2,1,0:T(8,128)(2,1)S(1)}, bf16[16,64,128]{2,1,0:T(8,128)(2,1)S(1)}, u32[]{:S(2)}, u32[]{:S(2)}) collective-permute-start(bf16[16,64,128]{2,1,0:T(8,128)(2,1)S(1)} %get-tuple-element.27), channel_id=1, source_target_pairs={{0,192},{32,224},{64,128},{96,160},{128,64},{160,96},{192,0},{224,... | collective-permute-start | bytes 786440 | tf_op jit(solution)/shard_map/ppermute | solution.py:337
  52.5 7.2 %collective-permute-start.5 = (bf16[16,64,128]{2,1,0:T(8,128)(2,1)S(1)}, bf16[16,64,128]{2,1,0:T(8,128)(2,1)S(1)}, u32[]{:S(2)}, u32[]{:S(2)}) collective-permute-start(bf16[16,64,128]{2,1,0:T(8,128)(2,1)S(1)} %get-tuple-element.28), channel_id=1, source_target_pairs={{0,64},{32,96},{64,0},{96,32},{128,192},{160,224},{192,128},{224,1... | collective-permute-start | bytes 786440 | tf_op jit(solution)/shard_map/ppermute | solution.py:336
  60.0 6.4 %collective-permute-start.8 = (bf16[16,64,128]{2,1,0:T(8,128)(2,1)S(1)}, bf16[16,64,128]{2,1,0:T(8,128)(2,1)S(1)}, u32[]{:S(2)}, u32[]{:S(2)}) collective-permute-start(bf16[16,64,128]{2,1,0:T(8,128)(2,1)S(1)} %get-tuple-element.21), channel_id=1, source_target_pairs={{0,64},{32,96},{64,0},{96,32},{128,192},{160,224},{192,128},{224,1... | collective-permute-start | bytes 786440 | tf_op jit(solution)/shard_map/ppermute | solution.py:340
  60.2 7.4 %copy-start.2 = (bf16[64,64,64]{2,1,0:T(8,128)(2,1)S(1)}, bf16[64,64,64]{2,1,0:T(8,128)(2,1)}, u32[]{:S(2)}) copy-start(bf16[64,64,64]{2,1,0:T(8,128)(2,1)} %smoother.11) | copy-start | bytes 1572868
  60.2 7.4 %collective-permute-start.7 = (bf16[16,64,128]{2,1,0:T(8,128)(2,1)S(1)}, bf16[16,64,128]{2,1,0:T(8,128)(2,1)S(1)}, u32[]{:S(2)}, u32[]{:S(2)}) collective-permute-start(bf16[16,64,128]{2,1,0:T(8,128)(2,1)S(1)} %get-tuple-element.25), channel_id=1, source_target_pairs={{0,192},{32,224},{64,128},{96,160},{128,64},{160,96},{192,0},{224,... | collective-permute-start | bytes 786440 | tf_op jit(solution)/shard_map/ppermute | solution.py:339
  66.2 11.6 %copy-start.5 = (s32[64,7]{0,1:T(8,128)S(1)}, s32[64,7]{0,1:T(8,128)}, u32[]{:S(2)}) copy-start(s32[64,7]{0,1:T(8,128)} %param.19) | copy-start | bytes 5380
  67.9 9.9 %collective-permute-start.9 = (bf16[32,64,128]{2,1,0:T(8,128)(2,1)S(1)}, bf16[32,64,128]{2,1,0:T(8,128)(2,1)S(1)}, u32[]{:S(2)}, u32[]{:S(2)}) collective-permute-start(bf16[32,64,128]{2,1,0:T(8,128)(2,1)S(1)} %get-tuple-element.18.own), channel_id=1, source_target_pairs={{2,1},{1,2},{4,3},{3,4},{6,5},{5,6},{8,7},{7,8},{10,9},{9,10},{12,... | collective-permute-start | bytes 1572872 | tf_op jit(solution)/shard_map/ppermute | solution.py:349
  69.8 8.0 %collective-permute-start.10 = (bf16[32,64,128]{2,1,0:T(8,128)(2,1)S(1)}, bf16[32,64,128]{2,1,0:T(8,128)(2,1)S(1)}, u32[]{:S(2)}, u32[]{:S(2)}) collective-permute-start(bf16[32,64,128]{2,1,0:T(8,128)(2,1)S(1)} %get-tuple-element.18.own), channel_id=1, source_target_pairs={{0,32},{32,0},{64,96},{96,64},{128,160},{160,128},{192,224},{224,1... | collective-permute-start | bytes 1572872 | tf_op jit(solution)/shard_map/ppermute | solution.py:351
  79.9 9.4 %collective-permute-start.11 = (f32[32,64,128]{2,1,0:T(8,128)S(1)}, f32[32,64,128]{2,1,0:T(8,128)S(1)}, u32[]{:S(2)}, u32[]{:S(2)}) collective-permute-start(f32[32,64,128]{2,1,0:T(8,128)S(1)} %coarse_second.1.kept), channel_id=1, source_target_pairs={{0,32},{32,0},{64,96},{96,64},{128,160},{160,128},{192,224},{224,1... | collective-permute-start | bytes 3145736 | tf_op jit(solution)/shard_map/ppermute | solution.py:361
